TPU v7x, 128 devices: a whole 4x4x4 slice. The times are simulated.
128 devices in a mesh: seq: 8 (over x_lo, z), fft: 16 (over y, x_hi, core).
Axes of the slice: x: 4 (x_hi: 2, x_lo: 2; x = x_hi * 2 + x_lo), y: 4, z: 4, core: 2. Of those that a mesh axis runs over, the one named last changes fastest.
Arguments:
- features: bfloat16 [256, 16384], P(None, ('seq', 'fft')), may hold values from -6 to 6
- sink_order: int32 [128, 128], P(('seq', 'fft')), may hold values from 0 to 127, each once within a row
- cotangent: bfloat16 [256, 16384], P(None, ('seq', 'fft')), may hold values from -6 to 6
- w_in: bfloat16 [768, 256], replicated, may hold values from -0.375 to 0.375
- short_taps: float32 [768, 3], replicated, may hold values from -1 to 1
- w_out: bfloat16 [256, 256], replicated, may hold values from -0.375 to 0.375
- filter_one: float32 [256, 16384], P(('seq', 'fft')), may hold values from -2 to 2
- filter_two: float32 [256, 16384], P(('seq', 'fft')), may hold values from -2 to 2
Outputs:
- grad_features: bfloat16 [256, 16384], P(None, ('seq', 'fft'))
- grad_w_in: float32 [768, 256], replicated
- grad_w_out: float32 [256, 256], replicated
- grad_short: float32 [768, 3], replicated
- grad_filter_one: float32 [256, 16384], P(('seq', 'fft'))
- grad_filter_two: float32 [256, 16384], P(('seq', 'fft'))
Inputs may be any that keep to these rules, and one draw needn't show every extreme that they name: Each row of sink_order names every position of a block of 128 sinks once.
All inputs are finite; a program needn't handle non-finite values.
Results may differ from a plain program's by a relative error of at most 0.0089.
Values may be sent and summed in bfloat16 or wider, within the bound.
A program may use at most 64 MiB of HBM per device.

v0:
```python
import math

import jax
import jax.numpy as jnp
from jax import lax
from jax.sharding import PartitionSpec as P

exact_mode = lax.Precision.HIGHEST
full_turn = 2.0 * math.pi


def from_behind(value, axis, steps):
    count = lax.axis_size(axis)
    first, last = (max(0, -steps), min(count, count - steps))
    return lax.ppermute(value, axis, [(source, source + steps) for source in range(first, last)])


def phase_grid(outer, inner, modulus):
    first = jnp.arange(outer, dtype=jnp.int32)[:, None]
    second = jnp.arange(inner, dtype=jnp.int32)[None, :]
    turns = first * second % modulus
    angles = turns.astype(jnp.float32) * (full_turn / modulus)
    return (jnp.cos(angles), jnp.sin(angles))


def complex_times(lower_real_part, left_imag, right_real, right_imag):
    return (
        lower_real_part * right_real - left_imag * right_imag,
        lower_real_part * right_imag + left_imag * right_real,
    )


def left_apply(table_real, table_imag, real_part, imag_part):
    form = "kn,...nm->...km"
    real_out = jnp.einsum(form, table_real, real_part, precision=exact_mode) - jnp.einsum(
        form, table_imag, imag_part, precision=exact_mode
    )
    imag_out = jnp.einsum(form, table_real, imag_part, precision=exact_mode) + jnp.einsum(
        form, table_imag, real_part, precision=exact_mode
    )
    return (real_out, imag_out)


def right_apply(real_part, imag_part, table_real, table_imag):
    form = "...n,nk->...k"
    real_out = jnp.einsum(form, real_part, table_real, precision=exact_mode) - jnp.einsum(
        form, imag_part, table_imag, precision=exact_mode
    )
    imag_out = jnp.einsum(form, imag_part, table_real, precision=exact_mode) + jnp.einsum(
        form, real_part, table_imag, precision=exact_mode
    )
    return (real_out, imag_out)


def forward_dft(real_part, imag_part):
    length = real_part.shape[-1]
    if length > 64 and length % 64 == 0:
        inner = length // 64
        leading = real_part.shape[:-1]
        real_grid = real_part.reshape(leading + (64, inner))
        imag_grid = imag_part.reshape(leading + (64, inner))
        cos_table, sin_table = phase_grid(64, 64, 64)
        real_grid, imag_grid = left_apply(cos_table, -sin_table, real_grid, imag_grid)
        twist_cos, twist_sin = phase_grid(64, inner, length)
        real_grid, imag_grid = complex_times(real_grid, imag_grid, twist_cos, -twist_sin)
        real_grid, imag_grid = forward_dft(real_grid, imag_grid)
        return (real_grid.reshape(leading + (length,)), imag_grid.reshape(leading + (length,)))
    cos_table, sin_table = phase_grid(length, length, length)
    return right_apply(real_part, imag_part, cos_table, -sin_table)


def inverse_dft(real_part, imag_part):
    length = real_part.shape[-1]
    if length > 64 and length % 64 == 0:
        inner = length // 64
        leading = real_part.shape[:-1]
        real_grid = real_part.reshape(leading + (64, inner))
        imag_grid = imag_part.reshape(leading + (64, inner))
        real_grid, imag_grid = inverse_dft(real_grid, imag_grid)
        twist_cos, twist_sin = phase_grid(64, inner, length)
        real_grid, imag_grid = complex_times(real_grid, imag_grid, twist_cos, twist_sin)
        cos_table, sin_table = phase_grid(64, 64, 64)
        real_grid, imag_grid = left_apply(cos_table, sin_table, real_grid, imag_grid)
        return (
            (real_grid / 64.0).reshape(leading + (length,)),
            (imag_grid / 64.0).reshape(leading + (length,)),
        )
    cos_table, sin_table = phase_grid(length, length, length)
    real_out, imag_out = right_apply(real_part, imag_part, cos_table, sin_table)
    return (real_out / length, imag_out / length)


def spectrum(signal):
    padded = jnp.concatenate([signal, jnp.zeros_like(signal)], axis=1)
    return forward_dft(padded, jnp.zeros_like(padded))


def to_time(spec_pair, length):
    real_out, unused = inverse_dft(spec_pair[0], spec_pair[1])
    return real_out[:, :length]


def spec_product(first, second):
    return complex_times(first[0], first[1], second[0], second[1])


def spec_conj_product(first, second):
    return complex_times(first[0], -first[1], second[0], second[1])


def local(features, sink_order, cotangent, w_in, short_taps, w_out, filter_one, filter_two):
    width = features.shape[0]
    row_count = features.shape[1]
    seq_count = lax.axis_size("seq")
    fft_count = lax.axis_size("fft")
    block_count = seq_count * fft_count
    channels = width // block_count
    length = filter_one.shape[1]
    scale = 1.0 / math.sqrt(length)
    order_local = sink_order[0]
    seq_input = jnp.take(features, order_local, axis=1)
    projected = jnp.dot(w_in, seq_input, preferred_element_type=jnp.float32)
    left_edge = from_behind(projected[:, row_count - 2 :], ("seq", "fft"), 1)
    padded_signal = jnp.concatenate([left_edge, projected], axis=1)
    mixed = short_taps[:, 0:1] * padded_signal[:, 2 : 2 + row_count]
    for offset in range(1, 3):
        mixed = (
            mixed
            + short_taps[:, offset : offset + 1]
            * padded_signal[:, 2 - offset : 2 - offset + row_count]
        )
    streams = mixed.astype(jnp.bfloat16)
    value_seq = streams[:width]
    gate_one_seq = streams[width : 2 * width]
    gate_two_seq = streams[2 * width :]
    out_grad = lax.dot_general(
        w_out, cotangent, (((0,), (0,)), ((), ())), preferred_element_type=jnp.float32
    ).astype(jnp.bfloat16)
    value_ch, gate_one_ch, gate_two_ch, out_grad_ch = (
        lax.all_to_all(
            value_seq.reshape(width, 1, row_count),
            ("seq", "fft"),
            split_axis=0,
            concat_axis=1,
            tiled=True,
        ),
        lax.all_to_all(
            gate_one_seq.reshape(width, 1, row_count),
            ("seq", "fft"),
            split_axis=0,
            concat_axis=1,
            tiled=True,
        ),
        lax.all_to_all(
            gate_two_seq.reshape(width, 1, row_count),
            ("seq", "fft"),
            split_axis=0,
            concat_axis=1,
            tiled=True,
        ),
        lax.all_to_all(
            out_grad.reshape(width, 1, row_count),
            ("seq", "fft"),
            split_axis=0,
            concat_axis=1,
            tiled=True,
        ),
    )
    value = value_ch.reshape(channels, length).astype(jnp.float32)
    gate_one = gate_one_ch.reshape(channels, length).astype(jnp.float32)
    gate_two = gate_two_ch.reshape(channels, length).astype(jnp.float32)
    out_gradf = out_grad_ch.reshape(channels, length).astype(jnp.float32)
    first_spec = spectrum(filter_one)
    second_spec = spectrum(filter_two)
    value_spec = spectrum(value)
    first_mix = to_time(spec_product(first_spec, value_spec), length)
    first_out = gate_one * first_mix
    first_out_spec = spectrum(first_out)
    second_mix = to_time(spec_product(second_spec, first_out_spec), length)
    second_out = (gate_two * second_mix).astype(jnp.bfloat16)
    grad_gate_two = (out_gradf * second_mix).astype(jnp.bfloat16)
    grad_second_mix = out_gradf * gate_two
    grad_second_spec = spectrum(grad_second_mix)
    grad_first_out = to_time(spec_conj_product(second_spec, grad_second_spec), length)
    grad_filter_two = to_time(spec_conj_product(first_out_spec, grad_second_spec), length) * scale
    grad_gate_one = (grad_first_out * first_mix).astype(jnp.bfloat16)
    grad_first_mix = grad_first_out * gate_one
    grad_first_spec = spectrum(grad_first_mix)
    grad_value = to_time(spec_conj_product(first_spec, grad_first_spec), length).astype(
        jnp.bfloat16
    )
    grad_filter_one = to_time(spec_conj_product(value_spec, grad_first_spec), length) * scale
    second_back, value_back, gate_one_back, gate_two_back = (
        lax.all_to_all(
            second_out.reshape(channels, block_count, row_count),
            ("seq", "fft"),
            split_axis=1,
            concat_axis=0,
            tiled=True,
        ),
        lax.all_to_all(
            grad_value.reshape(channels, block_count, row_count),
            ("seq", "fft"),
            split_axis=1,
            concat_axis=0,
            tiled=True,
        ),
        lax.all_to_all(
            grad_gate_one.reshape(channels, block_count, row_count),
            ("seq", "fft"),
            split_axis=1,
            concat_axis=0,
            tiled=True,
        ),
        lax.all_to_all(
            grad_gate_two.reshape(channels, block_count, row_count),
            ("seq", "fft"),
            split_axis=1,
            concat_axis=0,
            tiled=True,
        ),
    )
    second_seq = second_back.reshape(width, row_count)
    grad_streams = jnp.concatenate(
        [
            value_back.reshape(width, row_count),
            gate_one_back.reshape(width, row_count),
            gate_two_back.reshape(width, row_count),
        ],
        axis=0,
    )
    upper_boundary = from_behind(grad_streams[:, :2], ("seq", "fft"), -1)
    grad_extended = jnp.concatenate([grad_streams, upper_boundary], axis=1)
    grad_mixed = short_taps[:, 0:1] * grad_extended[:, 0:row_count]
    for offset in range(1, 3):
        grad_mixed = (
            grad_mixed
            + short_taps[:, offset : offset + 1] * grad_extended[:, offset : offset + row_count]
        )
    grad_projected = grad_mixed.astype(jnp.bfloat16)
    grad_streamsf = grad_streams.astype(jnp.float32)
    tap_terms = []
    for offset in range(3):
        tap_terms.append(
            jnp.sum(grad_streamsf * padded_signal[:, 2 - offset : 2 - offset + row_count], axis=1)
        )
    short_local = jnp.stack(tap_terms, axis=1)
    w_in_local = lax.dot_general(
        grad_projected, seq_input, (((1,), (1,)), ((), ())), preferred_element_type=jnp.float32
    )
    w_out_local = lax.dot_general(
        cotangent, second_seq, (((1,), (1,)), ((), ())), preferred_element_type=jnp.float32
    )
    w_in_total, w_out_total, short_total = lax.psum(
        (w_in_local, w_out_local, short_local), ("seq", "fft")
    )
    grad_seq = lax.dot_general(
        w_in, grad_projected, (((0,), (0,)), ((), ())), preferred_element_type=jnp.float32
    ).astype(jnp.bfloat16)
    grad_features = jnp.zeros_like(grad_seq).at[:, order_local].set(grad_seq)
    return (
        grad_features,
        w_in_total * scale,
        w_out_total * scale,
        short_total * scale,
        grad_filter_one,
        grad_filter_two,
    )


def solution(mesh):
    return jax.shard_map(
        local,
        mesh=mesh,
        in_specs=(
            P(None, ("seq", "fft")),
            P(("seq", "fft"), None),
            P(None, ("seq", "fft")),
            P(),
            P(),
            P(),
            P(("seq", "fft"), None),
            P(("seq", "fft"), None),
        ),
        out_specs=(
            P(None, ("seq", "fft")),
            P(),
            P(),
            P(),
            P(("seq", "fft"), None),
            P(("seq", "fft"), None),
        ),
        check_vma=False,
    )
```

profile of v0, /device:TPU:1, one launch (start us, length us, event | category | flops | bytes accessed | tf_op | source)
XLA Modules:
  0.0 450.6 jit_solution(17191482286439819632)
XLA Ops:
  9.1 11.5 %all-to-all-start = ((bf16[128,2,128]{2,1,0:T(2,128)(2,1)}), bf16[128,2,128]{2,1,0:T(2,128)(2,1)S(1)}, u32[]{:S(2)}, u32[]{:S(2)}) async-start(bf16[128,2,128]{2,1,0:T(2,128)(2,1)} %bitcast.592), calls=%async_computation | async-start | bytes 131072 | tf_op jit(solution)/shard_map/all_to_all | solution.py:161
  22.8 5.0 %collective-permute-start = (f32[768,2]{0,1:T(2,128)S(1)}, f32[768,2]{0,1:T(2,128)S(1)}, u32[]{:S(2)}, u32[]{:S(2)}) collective-permute-start(f32[768,2]{0,1:T(2,128)S(1)} %slice.80), channel_id=1, source_target_pairs={{0,1},{1,2},{2,3},{3,4},{4,5},{5,6},{6,7},{7,8},{8,9},{9,10},{10,1... | collective-permute-start | bytes 18440 | tf_op jit(solution)/shard_map/ppermute | solution.py:15
  34.5 8.2 %all-to-all-start.1 = ((bf16[128,2,128]{2,1,0:T(2,128)(2,1)}), bf16[128,2,128]{2,1,0:T(2,128)(2,1)S(1)}, u32[]{:S(2)}, u32[]{:S(2)}) async-start(bf16[128,2,128]{2,1,0:T(2,128)(2,1)} %bitcast.591), calls=%async_computation.1 | async-start | bytes 131072 | tf_op jit(solution)/shard_map/all_to_all | solution.py:154
  43.5 8.7 %all-to-all-done.1 = bf16[128,2,128]{2,1,0:T(2,128)(2,1)S(1)} async-done(((bf16[128,2,128]{2,1,0:T(2,128)(2,1)}), bf16[128,2,128]{2,1,0:T(2,128)(2,1)S(1)}, u32[]{:S(2)}, u32[]{:S(2)}) %all-to-all-start.1) | async-done | bytes 65568 | tf_op jit(solution)/shard_map/all_to_all | solution.py:154
  52.2 4.0 all-to-all-start.4
  57.3 8.6 %all-to-all-done.4 = bf16[128,2,128]{2,1,0:T(2,128)(2,1)S(1)} async-done(((bf16[128,2,128]{2,1,0:T(2,128)(2,1)}), bf16[128,2,128]{2,1,0:T(2,128)(2,1)S(1)}, u32[]{:S(2)}, u32[]{:S(2)}) %all-to-all-start.4) | async-done | bytes 65568 | tf_op jit(solution)/shard_map/all_to_all | solution.py:140
  65.9 4.3 all-to-all-start.2
  72.1 7.5 %all-to-all-done.2 = bf16[128,2,128]{2,1,0:T(2,128)(2,1)S(1)} async-done(((bf16[128,2,128]{2,1,0:T(2,128)(2,1)}), bf16[128,2,128]{2,1,0:T(2,128)(2,1)S(1)}, u32[]{:S(2)}, u32[]{:S(2)}) %all-to-all-start.2) | async-done | bytes 65568 | tf_op jit(solution)/shard_map/all_to_all | solution.py:147
  80.6 2.0 multiply_subtract_fusion.21
  84.4 1.5 fusion.306
  88.0 1.5 fusion.310
  92.8 1.5 fusion.32
  94.3 1.5 fusion.33
  97.2 1.5 fusion.294
  102.0 1.5 fusion.18
  103.5 1.5 fusion.19
  106.9 1.5 fusion.314
  115.2 1.7 fusion.116
  117.8 1.7 convolution_subtract_fusion.18
  121.3 1.7 convolution_add_fusion.20
  122.9 1.7 convolution_subtract_fusion.20
  131.0 1.8 multiply_subtract_fusion.8
  137.5 1.5 fusion.15
  139.0 2.0 copy.319
  149.0 1.5 fusion.290
  162.8 1.8 convolution_subtract_fusion.1
  173.3 1.5 fusion.27
  179.5 5.1 %all-to-all-start.5 = ((bf16[2,128,128]{2,0,1:T(2,128)(2,1)}), bf16[2,128,128]{2,0,1:T(2,128)(2,1)}, u32[]{:S(2)}, u32[]{:S(2)}) async-start(bf16[2,128,128]{2,0,1:T(2,128)(2,1)} %get-tuple-element.89), calls=%async_computation.5 | async-start | bytes 131072 | tf_op jit(solution)/shard_map/all_to_all | solution.py:208
  200.8 1.9 multiply_subtract_fusion
  204.1 1.5 fusion.3
  205.6 1.5 fusion.1
  207.1 2.1 copy.365
  210.4 2.0 copy.361
  212.4 1.9 copy.362
  214.4 1.6 fusion.154
  219.2 1.5 fusion.21
  220.7 1.5 fusion.23
  222.2 2.0 copy.293
  242.7 9.9 %all-to-all-start.3 = ((bf16[2,128,128]{2,0,1:T(2,128)(2,1)}), bf16[2,128,128]{2,0,1:T(2,128)(2,1)S(1)}, u32[]{:S(2)}, u32[]{:S(2)}) async-start(bf16[2,128,128]{2,0,1:T(2,128)(2,1)} %slice_bitcast_fusion.1), calls=%async_computation.3 | async-start | bytes 131072 | tf_op jit(solution)/shard_map/all_to_all | solution.py:201
  253.4 8.8 %all-to-all-done.3 = bf16[2,128,128]{2,0,1:T(2,128)(2,1)S(1)} async-done(((bf16[2,128,128]{2,0,1:T(2,128)(2,1)}), bf16[2,128,128]{2,0,1:T(2,128)(2,1)S(1)}, u32[]{:S(2)}, u32[]{:S(2)}) %all-to-all-start.3) | async-done | bytes 65568 | tf_op jit(solution)/shard_map/all_to_all | solution.py:201
  262.2 4.0 all-to-all-start.6
  267.9 7.9 %all-to-all-done.6 = bf16[2,128,128]{2,0,1:T(2,128)(2,1)S(1)} async-done(((bf16[2,128,128]{2,0,1:T(2,128)(2,1)}), bf16[2,128,128]{2,0,1:T(2,128)(2,1)S(1)}, u32[]{:S(2)}, u32[]{:S(2)}) %all-to-all-start.6) | async-done | bytes 65568 | tf_op jit(solution)/shard_map/all_to_all | solution.py:215
  275.9 4.0 all-to-all-start.7
  280.1 3.3 collective-permute-start.1
  283.4 6.2 %all-to-all-done.7 = bf16[2,128,128]{2,0,1:T(2,128)(2,1)S(1)} async-done(((bf16[2,128,128]{2,0,1:T(2,128)(2,1)}), bf16[2,128,128]{2,0,1:T(2,128)(2,1)S(1)}, u32[]{:S(2)}, u32[]{:S(2)}) %all-to-all-start.7) | async-done | bytes 65568 | tf_op jit(solution)/shard_map/all_to_all | solution.py:194
  295.4 64.5 %psum.23 = f32[768,3]{0,1:T(4,128)S(1)} all-reduce(f32[768,3]{0,1:T(4,128)S(1)} %pad_maximum_fusion.3), channel_id=1, replica_groups=mesh['seq'=8,'fft'=16] {'seq','fft'}, use_global_device_ids=true, to_apply=%region_6.7 | all-reduce | flops 2304 | bytes 18432 | tf_op jit(solution)/shard_map/psum | solution.py:254
  360.5 80.0 %all-reduce.9.cloned.1.call-done = (f32[768,256]{1,0:T(8,128)}, f32[256,256]{0,1:T(8,128)}) async-done(((f32[768,256]{1,0:T(8,128)}, f32[256,256]{0,1:T(8,128)}), (f32[768,256]{1,0:T(8,128)}, f32[256,256]{0,1:T(8,128)})) %all-reduce.9.cloned.1.call-update) | async-done | bytes 1048592 | tf_op jit(solution)/shard_map/psum | solution.py:254
  440.6 2.1 broadcast_multiply_fusion
  (327 shorter events, 132.0 us)
Async XLA Ops:
  7.2 15.0 %copy-start = (bf16[768,256]{1,0:T(8,128)(2,1)S(1)}, bf16[768,256]{1,0:T(8,128)(2,1)}, u32[]{:S(2)}) copy-start(bf16[768,256]{1,0:T(8,128)(2,1)} %param.11) | copy-start | bytes 1179652
  9.1 11.5 %copy-start.54 = (s32[1,128]{1,0:T(1,128)S(1)}, s32[1,128]{1,0:T(1,128)}, u32[]{:S(2)}) copy-start(s32[1,128]{1,0:T(1,128)} %param.9) | copy-start | bytes 1540
  9.1 12.1 %copy-start.49 = (bf16[256,128]{1,0:T(8,128)(2,1)S(1)}, bf16[256,128]{1,0:T(8,128)(2,1)}, u32[]{:S(2)}) copy-start(bf16[256,128]{1,0:T(8,128)(2,1)} %param.8) | copy-start | bytes 196612
  9.1 25.3 %all-to-all-start = ((bf16[128,2,128]{2,1,0:T(2,128)(2,1)}), bf16[128,2,128]{2,1,0:T(2,128)(2,1)S(1)}, u32[]{:S(2)}, u32[]{:S(2)}) async-start(bf16[128,2,128]{2,1,0:T(2,128)(2,1)} %bitcast.592), calls=%async_computation | async-start | bytes 131072 | tf_op jit(solution)/shard_map/all_to_all | solution.py:161
  22.8 10.3 %copy-start.8 = (f32[768,128]{0,1:T(8,128)}, f32[768,128]{0,1:T(8,128)S(1)}, u32[]{:S(2)}) copy-start(f32[768,128]{0,1:T(8,128)S(1)} %convolution_bitcast_fusion) | copy-start | bytes 1179652
  22.8 10.3 %collective-permute-start = (f32[768,2]{0,1:T(2,128)S(1)}, f32[768,2]{0,1:T(2,128)S(1)}, u32[]{:S(2)}, u32[]{:S(2)}) collective-permute-start(f32[768,2]{0,1:T(2,128)S(1)} %slice.80), channel_id=1, source_target_pairs={{0,1},{1,2},{2,3},{3,4},{4,5},{5,6},{6,7},{7,8},{8,9},{9,10},{10,1... | collective-permute-start | bytes 18440 | tf_op jit(solution)/shard_map/ppermute | solution.py:15
  34.5 17.7 %all-to-all-start.1 = ((bf16[128,2,128]{2,1,0:T(2,128)(2,1)}), bf16[128,2,128]{2,1,0:T(2,128)(2,1)S(1)}, u32[]{:S(2)}, u32[]{:S(2)}) async-start(bf16[128,2,128]{2,1,0:T(2,128)(2,1)} %bitcast.591), calls=%async_computation.1 | async-start | bytes 131072 | tf_op jit(solution)/shard_map/all_to_all | solution.py:154
  52.2 13.7 %all-to-all-start.4 = ((bf16[128,2,128]{2,1,0:T(2,128)(2,1)}), bf16[128,2,128]{2,1,0:T(2,128)(2,1)S(1)}, u32[]{:S(2)}, u32[]{:S(2)}) async-start(bf16[128,2,128]{2,1,0:T(2,128)(2,1)} %bitcast.593), calls=%async_computation.4 | async-start | bytes 131072 | tf_op jit(solution)/shard_map/all_to_all | solution.py:140
  57.2 13.5 %copy-start.30 = (f32[128,2,1,128]{3,0,1,2:T(8,128)}, f32[128,2,1,128]{3,0,1,2:T(8,128)S(1)}, u32[]{:S(2)}) copy-start(f32[128,2,1,128]{3,0,1,2:T(8,128)S(1)} %copy.552) | copy-start | bytes 393220
  57.3 13.5 %copy-start.41 = (bf16[256,1,128]{2,0,1:T(8,128)(2,1)}, bf16[256,1,128]{2,0,1:T(8,128)(2,1)S(1)}, u32[]{:S(2)}) copy-start(bf16[256,1,128]{2,0,1:T(8,128)(2,1)S(1)} %copy.254) | copy-start | bytes 196612
  65.9 13.7 %all-to-all-start.2 = ((bf16[128,2,128]{2,1,0:T(2,128)(2,1)}), bf16[128,2,128]{2,1,0:T(2,128)(2,1)S(1)}, u32[]{:S(2)}, u32[]{:S(2)}) async-start(bf16[128,2,128]{2,1,0:T(2,128)(2,1)} %bitcast.590), calls=%async_computation.2 | async-start | bytes 131072 | tf_op jit(solution)/shard_map/all_to_all | solution.py:147
  88.0 1.5 copy-start.34
  91.7 1.0 copy-start.23
  97.2 1.5 copy-start.33
  100.9 1.0 copy-start.24
  106.9 1.5 copy-start.32
  110.6 1.0 copy-start.21
  111.7 1.5 copy-start.17
  111.7 1.5 copy-start.19
  112.4 1.1 copy-start.14
  112.4 1.3 copy-start.15
  112.4 1.4 copy-start.16
  128.3 2.7 copy-start.4
  131.0 1.8 copy-start.6
  149.0 1.5 copy-start.38
  152.8 1.0 copy-start.22
  157.1 1.8 copy-start.28
  158.0 1.1 copy-start.25
  158.0 1.2 copy-start.26
  158.0 1.4 copy-start.27
  179.5 63.2 %all-to-all-start.5 = ((bf16[2,128,128]{2,0,1:T(2,128)(2,1)}), bf16[2,128,128]{2,0,1:T(2,128)(2,1)}, u32[]{:S(2)}, u32[]{:S(2)}) async-start(bf16[2,128,128]{2,0,1:T(2,128)(2,1)} %get-tuple-element.89), calls=%async_computation.5 | async-start | bytes 131072 | tf_op jit(solution)/shard_map/all_to_all | solution.py:208
  192.3 1.0 copy-start.5
  192.3 1.2 copy-start.7
  192.3 1.3 copy-start.29
  198.5 1.5 copy-start.13
  198.7 1.3 copy-start.18
  199.3 1.1 copy-start.3
  199.3 1.3 copy-start.11
  199.4 1.4 copy-start.12
  214.4 1.6 copy-start.10
  224.3 1.3 copy-start.20
  242.7 19.5 %all-to-all-start.3 = ((bf16[2,128,128]{2,0,1:T(2,128)(2,1)}), bf16[2,128,128]{2,0,1:T(2,128)(2,1)S(1)}, u32[]{:S(2)}, u32[]{:S(2)}) async-start(bf16[2,128,128]{2,0,1:T(2,128)(2,1)} %slice_bitcast_fusion.1), calls=%async_computation.3 | async-start | bytes 131072 | tf_op jit(solution)/shard_map/all_to_all | solution.py:201
  262.2 13.7 %all-to-all-start.6 = ((bf16[2,128,128]{2,0,1:T(2,128)(2,1)}), bf16[2,128,128]{2,0,1:T(2,128)(2,1)S(1)}, u32[]{:S(2)}, u32[]{:S(2)}) async-start(bf16[2,128,128]{2,0,1:T(2,128)(2,1)} %get-tuple-element.87), calls=%async_computation.6 | async-start | bytes 131072 | tf_op jit(solution)/shard_map/all_to_all | solution.py:215
  275.9 13.7 %all-to-all-start.7 = ((bf16[2,128,128]{2,0,1:T(2,128)(2,1)}), bf16[2,128,128]{2,0,1:T(2,128)(2,1)S(1)}, u32[]{:S(2)}, u32[]{:S(2)}) async-start(bf16[2,128,128]{2,0,1:T(2,128)(2,1)} %get-tuple-element.86), calls=%async_computation.7 | async-start | bytes 131072 | tf_op jit(solution)/shard_map/all_to_all | solution.py:194
  279.9 160.7 %all-reduce.9.cloned.1.call-start = ((), (), s32[]{:S(2)}) async-start(), calls=%async_computation.8 | async-start | bytes 2097152 | tf_op jit(solution)/shard_map/psum | solution.py:254
  280.0 9.5 %copy-start.46 = (bf16[256,128]{1,0:T(8,128)(2,1)S(1)}, bf16[256,128]{1,0:T(8,128)(2,1)}, u32[]{:S(2)}) copy-start(bf16[256,128]{1,0:T(8,128)(2,1)} %param.10) | copy-start | bytes 196612
  280.1 10.4 %collective-permute-start.1 = (bf16[768,2]{0,1:T(2,128)(2,1)S(1)}, bf16[768,2]{0,1:T(2,128)(2,1)S(1)}, u32[]{:S(2)}, u32[]{:S(2)}) collective-permute-start(bf16[768,2]{0,1:T(2,128)(2,1)S(1)} %slice.90), channel_id=1, source_target_pairs={{1,0},{2,1},{3,2},{4,3},{5,4},{6,5},{7,6},{8,7},{9,8},{10,9},{11,1... | collective-permute-start | bytes 9224 | tf_op jit(solution)/shard_map/ppermute | solution.py:15
  440.6 2.1 copy-start.45
  (18 other events, 15.0 us)
Sparse Core Ops, SparseCore 0:
  293.4 147.1 all-reduce.8
where the time goes:
time: 459 us; the launch traced here: 451 us
  waiting for transfers between devices  128 us (28%)
  matrix products  114 us (25%)
  blocking collectives  64.5 us (14%)
  local copies, waits for them, and re-layouts  60.5 us (13%)
  starting transfers between devices  59.4 us (13%)
  between operations  16.3 us (4%)
  other arithmetic  7.68 us (2%)
    psum x1, waiting for transfers between devices, local(): lax.psum((w_in_local, w_out_local, short_local), ('seq', 'fft'))  80 us
    psum x1, blocking collectives, local(): lax.psum((w_in_local, w_out_local, short_local), ('seq', 'fft'))  64.5 us
    dot_general x18, matrix products, left_apply(): jnp.einsum(form, table_imag, real_part, precision=exact_mode)  20.8 us
    dot_general x24, matrix products, left_apply(): jnp.einsum(form, table_real, real_part, precision=exact_mode)  16.5 us
    unnamed x128, local copies, waits for them, and re-layouts  16.2 us
    dot_general x19, matrix products, left_apply(): jnp.einsum(form, table_imag, imag_part, precision=exact_mode)  15.3 us
    dot_general x12, matrix products, right_apply(): jnp.einsum(form, real_part, table_imag, precision=exact_mode)  13.6 us
    dot_general x12, matrix products, right_apply(): jnp.einsum(form, imag_part, table_imag, precision=exact_mode)  12.6 us
  transfers between devices with their start and end apart: 11, of which 7 were waited for; matrix products, arithmetic and copies ran while one was open for 16% of the time, Pallas kernels for 0%

commit v1 on v0

v1 whole, which is shorter than its diff:
```python
import functools
import math

import jax
import jax.numpy as jnp
import ml_dtypes
import numpy as np
from jax import lax
from jax.experimental import pallas as pl
from jax.experimental.pallas import tpu as pltpu
from jax.sharding import PartitionSpec as P

bf16 = jnp.bfloat16
f32 = jnp.float32
LOGICAL = pl.DeviceIdType.LOGICAL


def table_halves(table):
    high = table.astype(ml_dtypes.bfloat16)
    low = (table - high.astype(np.float64)).astype(ml_dtypes.bfloat16)
    return high, low


def transform_tables(blocks, lanes):
    length = blocks * lanes
    shift = 0.25
    row = np.arange(blocks, dtype=np.float64)
    lane = np.arange(lanes, dtype=np.float64)
    outer = -2.0 * np.pi * np.outer(row + shift, row) / blocks
    twist = -2.0 * np.pi * np.outer(row + shift, lane) / length
    inner = -2.0 * np.pi * (np.outer(lane, lane) % lanes) / lanes
    first = np.concatenate([np.cos(outer), np.sin(outer)], axis=0)
    second = np.block(
        [[np.cos(inner), np.sin(inner)], [-np.sin(inner), np.cos(inner)]]
    )
    second_back = second.T
    first_back = np.concatenate([np.cos(outer).T, np.sin(outer).T], axis=1) / length
    twiddle = np.concatenate([np.cos(twist), np.sin(twist)], axis=1).astype(np.float32)
    return (
        *table_halves(first),
        *table_halves(second),
        *table_halves(second_back),
        *table_halves(first_back),
        twiddle,
    )


def halves(x):
    high = x.astype(bf16)
    return high, (x - high.astype(f32)).astype(bf16)


def dot(a, b):
    return jnp.dot(a, b, preferred_element_type=f32)


def dot_nt(a, b):
    return lax.dot_general(a, b, (((1,), (1,)), ((), ())), preferred_element_type=f32)


def dot_tn(a, b):
    return lax.dot_general(a, b, (((0,), (0,)), ((), ())), preferred_element_type=f32)


def dot3(left, right):
    return dot(left[0], right[0]) + (dot(left[0], right[1]) + dot(left[1], right[0]))


def kernel(
    count,
    fft_size,
    feat_ref,
    order_ref,
    cot_ref,
    win_ref,
    taps_ref,
    wout_ref,
    filt1_ref,
    filt2_ref,
    t1h,
    t1l,
    t2h,
    t2l,
    u2h,
    u2l,
    u1h,
    u1l,
    tw_ref,
    gfeat_ref,
    gwin_ref,
    gwout_ref,
    gshort_ref,
    gf1_ref,
    gf2_ref,
    stage_a,
    stage_b,
    seq_scr,
    send1,
    recv1,
    send2,
    recv2,
    send3,
    recv3,
    slab,
    recv4,
    short_slab,
    recv_short,
    send_sem,
    recv_sem,
):
    blocks = count
    lanes = 128
    width = 2 * count
    me = lax.axis_index("seq") * fft_size + lax.axis_index("fft")
    scale = 1.0 / math.sqrt(blocks * lanes)

    barrier = pltpu.get_barrier_semaphore()

    def greet(i, carry):
        pl.semaphore_signal(
            barrier, inc=1, device_id=lax.rem(me + i, count), device_id_type=LOGICAL
        )
        return carry

    lax.fori_loop(1, count, greet, 0)

    def exchange(source, target, phase):
        def one(i, carry):
            peer = lax.rem(me + i, count)
            pltpu.make_async_remote_copy(
                source(peer),
                target.at[me],
                send_sem.at[phase],
                recv_sem.at[phase],
                device_id=peer,
                device_id_type=LOGICAL,
            ).start()
            return carry

        lax.fori_loop(1, count, one, 0)
        pltpu.make_async_copy(source(me), target.at[me], recv_sem.at[phase]).start()

    def arrived(target, phase):
        pltpu.make_async_copy(target, target, recv_sem.at[phase]).wait()

    def sent(target, phase):
        part = target.at[pl.ds(0, count - 1)]
        pltpu.make_async_copy(part, part, send_sem.at[phase]).wait()

    order = order_ref[...]
    pick = jnp.where(
        lax.broadcasted_iota(jnp.int32, (lanes, lanes), 0) == order, 1.0, 0.0
    ).astype(bf16)
    seq_scr[...] = dot(feat_ref[...], pick).astype(bf16)
    stage_a[0 : 3 * width, :] = dot(win_ref[...], seq_scr[...])
    stage_a[3 * width : 4 * width, :] = dot_tn(wout_ref[...], cot_ref[...])
    for s in range(4):
        for c in range(2):
            stage_b[pl.ds(2 * s + c, count, stride=8), :] = stage_a[
                pl.ds(width * s + c, count, stride=2), :
            ]
    send1[...] = stage_b[...].reshape(count, 8, lanes).astype(bf16)

    pl.semaphore_wait(barrier, count - 1)
    exchange(lambda peer: send1.at[peer], recv1, 0)

    twr = tw_ref[:, 0:lanes]
    twi = tw_ref[:, lanes : 2 * lanes]
    first = (t1h[...], t1l[...])
    second = (t2h[...], t2l[...])
    second_back = (u2h[...], u2l[...])
    first_back = (u1h[...], u1l[...])

    def forward(signals):
        data = halves(jnp.concatenate(signals, axis=1))
        mid = dot3(first, data)
        rows = []
        for i in range(len(signals)):
            re = mid[0:blocks, i * lanes : (i + 1) * lanes]
            im = mid[blocks : 2 * blocks, i * lanes : (i + 1) * lanes]
            rows.append(
                jnp.concatenate([re * twr - im * twi, re * twi + im * twr], axis=1)
            )
        out = dot3(halves(jnp.concatenate(rows, axis=0)), second)
        return [out[i * blocks : (i + 1) * blocks, :] for i in range(len(signals))]

    def backward(spectra):
        mid = dot3(halves(jnp.concatenate(spectra, axis=0)), second_back)
        columns = []
        for i in range(len(spectra)):
            re = mid[i * blocks : (i + 1) * blocks, 0:lanes]
            im = mid[i * blocks : (i + 1) * blocks, lanes : 2 * lanes]
            columns.append(
                jnp.concatenate([re * twr + im * twi, im * twr - re * twi], axis=0)
            )
        out = dot3(first_back, halves(jnp.concatenate(columns, axis=1)))
        return [out[:, i * lanes : (i + 1) * lanes] for i in range(len(spectra))]

    def times(a, b):
        ar, ai = a[:, 0:lanes], a[:, lanes : 2 * lanes]
        br, bi = b[:, 0:lanes], b[:, lanes : 2 * lanes]
        return jnp.concatenate([ar * br - ai * bi, ar * bi + ai * br], axis=1)

    def conj_times(a, b):
        ar, ai = a[:, 0:lanes], a[:, lanes : 2 * lanes]
        br, bi = b[:, 0:lanes], b[:, lanes : 2 * lanes]
        return jnp.concatenate([ar * br + ai * bi, ar * bi - ai * br], axis=1)

    lane_id = lax.broadcasted_iota(jnp.int32, (blocks, lanes), 1)
    row_id = lax.broadcasted_iota(jnp.int32, (blocks, lanes), 0)

    def earlier(x, steps):
        turned = pltpu.roll(x, steps, 1)
        above = jnp.where(row_id == 0, 0.0, pltpu.roll(turned, 1, 0))
        return jnp.where(lane_id < steps, above, turned)

    def later(x, steps):
        turned = pltpu.roll(x, lanes - steps, 1)
        below = jnp.where(row_id == blocks - 1, 0.0, pltpu.roll(turned, blocks - 1, 0))
        return jnp.where(lane_id >= lanes - steps, below, turned)

    filters = [
        ref[pl.ds(c, count, stride=2), :] for ref in (filt1_ref, filt2_ref) for c in range(2)
    ]
    spec_f = forward(filters)
    spec_f1, spec_f2 = spec_f[0:2], spec_f[2:4]

    arrived(recv1, 0)
    stage_b[...] = recv1[...].astype(f32).reshape(count * 8, lanes)

    def tap(s, c, k):
        return taps_ref[pl.ds(width * s + 2 * me + c, 1), k : k + 1]

    shifted = []
    streams = []
    for s in range(3):
        for c in range(2):
            now = stage_b[pl.ds(2 * s + c, count, stride=8), :]
            moved = [now, earlier(now, 1), earlier(now, 2)]
            mixed = tap(s, c, 0) * now
            for k in range(1, 3):
                mixed = mixed + tap(s, c, k) * moved[k]
            shifted.append(moved)
            streams.append(mixed.astype(bf16).astype(f32))
    value, gate_one, gate_two = streams[0:2], streams[2:4], streams[4:6]
    out_grad = [stage_b[pl.ds(6 + c, count, stride=8), :] for c in range(2)]
    grad_second_mix = [out_grad[c] * gate_two[c] for c in range(2)]

    spec = forward(value + grad_second_mix)
    spec_value, spec_gsm = spec[0:2], spec[2:4]
    mixes = backward(
        [times(spec_f1[c], spec_value[c]) for c in range(2)]
        + [conj_times(spec_f2[c], spec_gsm[c]) for c in range(2)]
    )
    first_mix, grad_first_out = mixes[0:2], mixes[2:4]
    first_out = [gate_one[c] * first_mix[c] for c in range(2)]
    grad_first_mix = [gate_one[c] * grad_first_out[c] for c in range(2)]
    spec = forward(first_out + grad_first_mix)
    spec_fo, spec_gfm = spec[0:2], spec[2:4]
    mixes = backward(
        [times(spec_f2[c], spec_fo[c]) for c in range(2)]
        + [conj_times(spec_f1[c], spec_gfm[c]) for c in range(2)]
    )
    second_mix, grad_value = mixes[0:2], mixes[2:4]
    grad_streams = (
        [g.astype(bf16).astype(f32) for g in grad_value]
        + [(grad_first_out[c] * first_mix[c]).astype(bf16).astype(f32) for c in range(2)]
        + [(out_grad[c] * second_mix[c]).astype(bf16).astype(f32) for c in range(2)]
    )
    for s in range(3):
        for c in range(2):
            g = grad_streams[2 * s + c]
            total = tap(s, c, 0) * g
            for k in range(1, 3):
                total = total + tap(s, c, k) * later(g, k)
            stage_a[pl.ds(2 * s + c, count, stride=8), :] = total
    for c in range(2):
        stage_a[pl.ds(6 + c, count, stride=8), :] = gate_two[c] * second_mix[c]
    send2[...] = stage_a[...].reshape(count, 8, lanes).astype(bf16)
    exchange(lambda peer: send2.at[peer], recv2, 1)

    line = jnp.zeros((1, lanes), f32)
    short_lane = lax.broadcasted_iota(jnp.int32, (1, lanes), 1)
    for j in range(6):
        for k in range(3):
            part = jnp.sum(grad_streams[j] * shifted[j][k], axis=0, keepdims=True)
            part = jnp.sum(part, axis=1, keepdims=True)
            line = jnp.where(short_lane == 3 * j + k, part * scale, line)
    short_slab[...] = line
    exchange(lambda peer: short_slab, recv_short, 2)
    grads = backward(
        [conj_times(spec_value[c], spec_gfm[c]) for c in range(2)]
        + [conj_times(spec_fo[c], spec_gsm[c]) for c in range(2)]
    )
    for c in range(2):
        gf1_ref[pl.ds(c, count, stride=2), :] = grads[c] * scale
        gf2_ref[pl.ds(c, count, stride=2), :] = grads[2 + c] * scale

    arrived(recv2, 1)
    stage_b[...] = recv2[...].astype(f32).reshape(count * 8, lanes)
    rows = stage_b[...].astype(bf16)
    with_seq = dot_nt(rows, seq_scr[...])
    with_cot = dot_nt(rows, cot_ref[...])
    kind = lax.broadcasted_iota(jnp.int32, (count * 8, 256), 0) % 8
    partial = jnp.where(kind < 6, with_seq, with_cot) * scale
    send3[...] = partial.reshape(count, 8, 256).astype(bf16)
    exchange(lambda peer: send3.at[peer], recv3, 3)

    for s in range(3):
        for c in range(2):
            stage_a[pl.ds(width * s + c, count, stride=2), :] = stage_b[
                pl.ds(2 * s + c, count, stride=8), :
            ]
    grad_projected = stage_a[0 : 3 * width, :].astype(bf16)
    grad_seq = dot_tn(win_ref[...], grad_projected).astype(bf16)
    gfeat_ref[...] = dot_nt(grad_seq, pick).astype(bf16)

    arrived(recv3, 3)
    slab[...] = jnp.sum(recv3[...].astype(f32), axis=0).astype(bf16)
    exchange(lambda peer: slab, recv4, 4)
    arrived(recv_short, 2)
    gathered = recv_short[...].reshape(count, lanes)
    for s in range(3):
        for c in range(2):
            j = 2 * s + c
            gshort_ref[pl.ds(width * s + c, count, stride=2), :] = gathered[:, 3 * j : 3 * j + 3]
    arrived(recv4, 4)
    total = recv4[...].astype(f32).reshape(count * 8, 256)
    for h in range(2):
        stage_b[...] = total[:, h * lanes : (h + 1) * lanes]
        for s in range(4):
            for c in range(2):
                stage_a[pl.ds(width * s + c, count, stride=2), :] = stage_b[
                    pl.ds(2 * s + c, count, stride=8), :
                ]
        gwin_ref[:, h * lanes : (h + 1) * lanes] = stage_a[0 : 3 * width, :]
        gwout_ref[h * lanes : (h + 1) * lanes, :] = stage_a[3 * width : 4 * width, :].T

    sent(send1, 0)
    sent(send2, 1)
    sent(recv_short, 2)
    sent(send3, 3)
    sent(recv4, 4)


def local(
    count, fft_size, features, sink_order, cotangent, w_in, short_taps, w_out, filter_one, filter_two
):
    width, lanes = features.shape
    length = filter_one.shape[1]
    tables = [jnp.asarray(t) for t in transform_tables(count, lanes)]

    def by_row(filt):
        return filt.reshape(2, count, lanes).transpose(1, 0, 2).reshape(2 * count, lanes)

    def by_channel(grad):
        return grad.reshape(count, 2, lanes).transpose(1, 0, 2).reshape(2, length)

    vmem = pl.BlockSpec(memory_space=pltpu.VMEM)
    shape = jax.ShapeDtypeStruct
    out = pl.pallas_call(
        functools.partial(kernel, count, fft_size),
        out_shape=(
            shape((width, lanes), bf16),
            shape((3 * width, width), f32),
            shape((width, width), f32),
            shape((3 * width, 3), f32),
            shape((width, lanes), f32),
            shape((width, lanes), f32),
        ),
        in_specs=[vmem] * 17,
        out_specs=(vmem,) * 6,
        scratch_shapes=[
            pltpu.VMEM((8 * count, lanes), f32),
            pltpu.VMEM((8 * count, lanes), f32),
            pltpu.VMEM((width, lanes), bf16),
            pltpu.VMEM((count, 8, lanes), bf16),
            pltpu.VMEM((count, 8, lanes), bf16),
            pltpu.VMEM((count, 8, lanes), bf16),
            pltpu.VMEM((count, 8, lanes), bf16),
            pltpu.VMEM((count, 8, width), bf16),
            pltpu.VMEM((count, 8, width), bf16),
            pltpu.VMEM((8, width), bf16),
            pltpu.VMEM((count, 8, width), bf16),
            pltpu.VMEM((1, lanes), f32),
            pltpu.VMEM((count, 1, lanes), f32),
            pltpu.SemaphoreType.DMA((5,)),
            pltpu.SemaphoreType.DMA((5,)),
        ],
        compiler_params=pltpu.CompilerParams(collective_id=0, has_side_effects=True),
    )(
        features,
        sink_order,
        cotangent,
        w_in,
        short_taps,
        w_out,
        by_row(filter_one),
        by_row(filter_two),
        *tables,
    )
    gfeat, gwin, gwout, gshort, gf1, gf2 = out
    return gfeat, gwin, gwout, gshort, by_channel(gf1), by_channel(gf2)


def solution(mesh):
    count = mesh.shape["seq"] * mesh.shape["fft"]
    both = ("seq", "fft")
    return jax.shard_map(
        functools.partial(local, count, mesh.shape["fft"]),
        mesh=mesh,
        in_specs=(
            P(None, both),
            P(both, None),
            P(None, both),
            P(),
            P(),
            P(),
            P(both, None),
            P(both, None),
        ),
        out_specs=(P(None, both), P(), P(), P(), P(both, None), P(both, None)),
        check_vma=False,
    )
```

time: 459 us -> 63.6 us (0.14); the launches traced: 451 us -> 63.3 us
  waiting for transfers between devices: 128 us -> 0 us
  matrix products: 114 us -> 0 us
  blocking collectives: 64.5 us -> 0 us
  starting transfers between devices: 59.4 us -> 0 us
  Pallas kernels: 0 us -> 53.9 us
  local copies, waits for them, and re-layouts: 60.5 us -> 8.76 us
  between operations: 16.3 us -> 0.65 us
  other arithmetic: 7.68 us -> 0 us
    dot_general x127 -> x0, matrix products: 114 us -> none  [the longest x18 20.8 us: left_apply(): jnp.einsum(form, table_imag, real_part, precision=exact_mode)]
    psum x1 -> x0, waiting for transfers between devices: 80 us -> none  [local(): lax.psum((w_in_local, w_out_local, short_local), ('seq', 'fft'))]
    psum x1 -> x0, blocking collectives: 64.5 us -> none  [local(): lax.psum((w_in_local, w_out_local, short_local), ('seq', 'fft'))]
    pallas_call x0 -> x1, Pallas kernels: none -> 53.9 us  [local(): pl.pallas_call(functools.partial(kernel, count, fft_size), out_shape=(sha...]
    all_to_all x8 -> x0, starting transfers between devices: 51 us -> none  [the longest x1 11.5 us: local(): lax.all_to_all(out_grad.reshape(width, 1, row_count), ('seq', 'fft'), spl...]
    all_to_all x8 -> x0, waiting for transfers between devices: 47.8 us -> none  [the longest x1 8.79 us: local(): lax.all_to_all(grad_value.reshape(channels, block_count, row_count), ('se...]
    reshape x33 -> x0, local copies, waits for them, and re-layouts: 19.7 us -> none  [the longest x6 6 us: inverse_dft(): (real_grid / 64.0).reshape(leading + (length,))]
    div x12 -> x0, local copies, waits for them, and re-layouts: 13.6 us -> none  [the longest x6 6.81 us: inverse_dft(): imag_grid / 64.0]
  transfers between devices with their start and end apart: 11 -> 0, of which waited for: 7 -> 0; matrix products, arithmetic and copies ran while one was open for 16% -> 0% of each run, Pallas kernels for 0% -> 0%
where the time goes in v1:
time: 63.6 us; the launch traced here: 63.3 us
  Pallas kernels  53.9 us (85%)
  local copies, waits for them, and re-layouts  8.76 us (14%)
  between operations  0.65 us (1%)
    pallas_call x1, Pallas kernels, local(): pl.pallas_call(functools.partial(kernel, count, fft_size), out_shape=(sha...  53.9 us
    unnamed x15, local copies, waits for them, and re-layouts  8.76 us

profile of v1, /device:TPU:1, one launch (start us, length us, event | category | flops | bytes accessed | tf_op | source)
XLA Modules:
  0.0 63.3 jit_solution(4316131870172964560)
XLA Ops:
  0.6 1.6 %copy.25.taps_ref = f32[768,3]{1,0:T(8,128)} copy(f32[768,3]{0,1:T(4,128)} %param.21) | data formatting | bytes 18432 | tf_op args[4]
  2.3 53.9 %shard_map.208 = (bf16[256,128]{1,0:T(8,128)(2,1)}, f32[768,256]{1,0:T(8,128)}, f32[256,256]{1,0:T(8,128)}, f32[768,3]{1,0:T(8,128)}, f32[256,128]{1,0:T(8,128)}, /*index=5*/f32[256,128]{1,0:T(8,128)}) custom-call(bf16[256,128]{1,0:T(8,128)(2,1)} %feat_ref.1, s32[1,128]{1,0:T(1,128)} %order_ref.1, bf16[256,128]{1,0:T(8,128)(2,1)} %cot_ref.1, ...), custom_call_target="tpu_custom_call" | custom-call | tf_op jit(solution)/shard_map/pallas_call | solution.py:361
  56.2 0.0 copy-start.3
  56.2 1.8 %copy.28 = f32[768,3]{0,1:T(4,128)} copy(f32[768,3]{1,0:T(8,128)} %get-tuple-element.21) | data formatting | bytes 18432
  58.0 0.0 copy-done.3
  58.0 0.6 copy.34
  58.6 0.0 copy-start
  58.6 2.1 %copy.35 = f32[768,256]{1,0:T(8,128)} copy(f32[768,256]{1,0:T(8,128)} %get-tuple-element.31) | data formatting | bytes 1572864
  60.7 0.0 copy-done
  60.7 0.0 copy-start.2
  60.7 0.7 %copy.36 = f32[256,256]{1,0:T(8,128)} copy(f32[256,256]{1,0:T(8,128)S(1)} %copy-done) | data formatting | bytes 524288
  61.4 0.3 copy-done.2
  61.7 0.0 copy-start.1
  61.7 0.7 %copy.37 = f32[2,16384]{1,0:T(2,128)} copy(f32[2,16384]{1,0:T(2,128)S(1)} %bitcast.23) | data formatting | bytes 262144
  62.4 0.3 copy-done.1
  62.7 0.7 %copy.38 = f32[2,16384]{1,0:T(2,128)} copy(f32[2,16384]{1,0:T(2,128)S(1)} %bitcast.22) | data formatting | bytes 262144
Async XLA Ops:
  56.2 1.8 %copy-start.3 = (bf16[256,128]{1,0:T(8,128)(2,1)S(1)}, bf16[256,128]{1,0:T(8,128)(2,1)}, u32[]{:S(2)}) copy-start(bf16[256,128]{1,0:T(8,128)(2,1)} %get-tuple-element.30) | copy-start | bytes 196612
  58.6 2.1 %copy-start = (f32[256,256]{1,0:T(8,128)S(1)}, f32[256,256]{1,0:T(8,128)}, u32[]{:S(2)}) copy-start(f32[256,256]{1,0:T(8,128)} %get-tuple-element.32) | copy-start | bytes 786436
  60.7 1.0 %copy-start.2 = (f32[256,128]{1,0:T(8,128)S(1)}, f32[256,128]{1,0:T(8,128)}, u32[]{:S(2)}) copy-start(f32[256,128]{1,0:T(8,128)} %get-tuple-element.16) | copy-start | bytes 393220
  61.7 1.0 %copy-start.1 = (f32[256,128]{1,0:T(8,128)S(1)}, f32[256,128]{1,0:T(8,128)}, u32[]{:S(2)}) copy-start(f32[256,128]{1,0:T(8,128)} %get-tuple-element.17) | copy-start | bytes 393220

commit v2 on v1

--- a/solution.py
+++ b/solution.py
@@ -13,6 +13,12 @@
 bf16 = jnp.bfloat16
 f32 = jnp.float32
 LOGICAL = pl.DeviceIdType.LOGICAL
+SIDE = 4
+
+
+def chip_offsets():
+    steps = [(a, b, c) for a in range(SIDE) for b in range(SIDE) for c in range(SIDE) if a + b + c]
+    return sorted(steps, key=lambda step: -sum(min(d, SIDE - d) for d in step))
 
 
 def table_halves(table):
@@ -36,13 +42,10 @@
     second_back = second.T
     first_back = np.concatenate([np.cos(outer).T, np.sin(outer).T], axis=1) / length
     twiddle = np.concatenate([np.cos(twist), np.sin(twist)], axis=1).astype(np.float32)
-    return (
-        *table_halves(first),
-        *table_halves(second),
-        *table_halves(second_back),
-        *table_halves(first_back),
-        twiddle,
-    )
+    pieces = [np.concatenate(table_halves(first), axis=1)]
+    for table in (second, second_back, first_back):
+        pieces.extend(table_halves(table))
+    return np.concatenate(pieces, axis=0), twiddle
 
 
 def halves(x):
@@ -68,92 +71,134 @@
 
 def kernel(
     count,
-    fft_size,
+    feat_in,
+    order_in,
+    cot_in,
+    win_in,
+    wout_in,
+    taps_in,
+    filt1_in,
+    filt2_in,
+    tab_in,
+    tw_in,
+    sums_out,
+    short_out,
+    gfeat_out,
+    gf1_out,
+    gf2_out,
     feat_ref,
     order_ref,
-    cot_ref,
+    cot_pair,
     win_ref,
+    wout_ref,
     taps_ref,
-    wout_ref,
     filt1_ref,
     filt2_ref,
-    t1h,
-    t1l,
-    t2h,
-    t2l,
-    u2h,
-    u2l,
-    u1h,
-    u1l,
+    tab_ref,
     tw_ref,
     gfeat_ref,
-    gwin_ref,
-    gwout_ref,
-    gshort_ref,
     gf1_ref,
     gf2_ref,
     stage_a,
     stage_b,
-    seq_scr,
+    seq_pair,
     send1,
     recv1,
     send2,
     recv2,
+    other_rows,
     send3,
     recv3,
     slab,
-    recv4,
+    sums,
     short_slab,
-    recv_short,
+    shorts,
+    in_sem,
+    out_sem,
     send_sem,
     recv_sem,
 ):
     blocks = count
+    chips = count // 2
     lanes = 128
     width = 2 * count
-    me = lax.axis_index("seq") * fft_size + lax.axis_index("fft")
     scale = 1.0 / math.sqrt(blocks * lanes)
 
+    seq_index = lax.axis_index("seq")
+    fft_index = lax.axis_index("fft")
+    core = fft_index % 2
+    x = (fft_index // 2) % 2 * 2 + seq_index // SIDE
+    y = fft_index // SIDE
+    z = seq_index % SIDE
+    along_x = [(x + d) % SIDE % 2 * 32 + (x + d) % SIDE // 2 for d in range(SIDE)]
+    along_y = [(y + d) % SIDE * 2 for d in range(SIDE)]
+    along_z = [(z + d) % SIDE * 8 for d in range(SIDE)]
+    chip = along_x[0] + along_y[0] + along_z[0]
+    me = 2 * chip + core
+    sibling = 2 * chip + (1 - core)
+    other_chips = [along_x[a] + along_y[b] + along_z[c] for a, b, c in chip_offsets()]
+
+    loads = [
+        pltpu.make_async_copy(source, target, in_sem.at[n])
+        for n, (source, target) in enumerate(
+            (
+                (feat_in, feat_ref),
+                (order_in, order_ref),
+                (cot_in, cot_pair.at[core]),
+                (win_in, win_ref),
+                (wout_in, wout_ref),
+                (taps_in, taps_ref),
+                (filt1_in, filt1_ref),
+                (filt2_in, filt2_ref),
+                (tab_in, tab_ref),
+                (tw_in, tw_ref),
+            )
+        )
+    ]
+    for load in loads:
+        load.start()
     barrier = pltpu.get_barrier_semaphore()
-
-    def greet(i, carry):
-        pl.semaphore_signal(
-            barrier, inc=1, device_id=lax.rem(me + i, count), device_id_type=LOGICAL
+    for peer_chip in other_chips:
+        for c in range(2):
+            pl.semaphore_signal(
+                barrier, inc=1, device_id=2 * peer_chip + c, device_id_type=LOGICAL
+            )
+    pl.semaphore_signal(barrier, inc=1, device_id=sibling, device_id_type=LOGICAL)
+
+    def send(source, target, phase, peer):
+        copy = pltpu.make_async_remote_copy(
+            source,
+            target,
+            send_sem.at[phase],
+            recv_sem.at[phase],
+            device_id=peer,
+            device_id_type=LOGICAL,
         )
-        return carry
-
-    lax.fori_loop(1, count, greet, 0)
+        copy.start()
+        return copy
 
     def exchange(source, target, phase):
-        def one(i, carry):
-            peer = lax.rem(me + i, count)
-            pltpu.make_async_remote_copy(
-                source(peer),
-                target.at[me],
-                send_sem.at[phase],
-                recv_sem.at[phase],
-                device_id=peer,
-                device_id_type=LOGICAL,
-            ).start()
-            return carry
-
-        lax.fori_loop(1, count, one, 0)
-        pltpu.make_async_copy(source(me), target.at[me], recv_sem.at[phase]).start()
-
-    def arrived(target, phase):
-        pltpu.make_async_copy(target, target, recv_sem.at[phase]).wait()
-
-    def sent(target, phase):
-        part = target.at[pl.ds(0, count - 1)]
+        for peer_chip in other_chips:
+            send(source(peer_chip), target, phase, 2 * peer_chip + core)
+        pltpu.make_async_copy(source(chip), target, recv_sem.at[phase]).start()
+
+    def arrived(whole, phase):
+        pltpu.make_async_copy(whole, whole, recv_sem.at[phase]).wait()
+
+    def sent(whole, phase):
+        part = whole.at[pl.ds(0, whole.shape[0] - 1)]
         pltpu.make_async_copy(part, part, send_sem.at[phase]).wait()
 
+    for n in range(5):
+        loads[n].wait()
     order = order_ref[...]
     pick = jnp.where(
         lax.broadcasted_iota(jnp.int32, (lanes, lanes), 0) == order, 1.0, 0.0
     ).astype(bf16)
-    seq_scr[...] = dot(feat_ref[...], pick).astype(bf16)
-    stage_a[0 : 3 * width, :] = dot(win_ref[...], seq_scr[...])
-    stage_a[3 * width : 4 * width, :] = dot_tn(wout_ref[...], cot_ref[...])
+    seq_input = dot(feat_ref[...], pick).astype(bf16)
+    seq_pair[core] = seq_input
+    stage_a[0 : 3 * width, :] = dot(win_ref[...], seq_input)
+    stage_a[3 * width : 4 * width, :] = dot_tn(wout_ref[...], cot_pair[core])
     for s in range(4):
         for c in range(2):
             stage_b[pl.ds(2 * s + c, count, stride=8), :] = stage_a[
@@ -162,18 +207,29 @@
     send1[...] = stage_b[...].reshape(count, 8, lanes).astype(bf16)
 
     pl.semaphore_wait(barrier, count - 1)
-    exchange(lambda peer: send1.at[peer], recv1, 0)
-
+    for peer_chip in other_chips:
+        for c in range(2):
+            peer = 2 * peer_chip + c
+            send(send1.at[peer], recv1.at[me], 0, peer)
+    send(send1.at[sibling], recv1.at[me], 0, sibling)
+    pltpu.make_async_copy(send1.at[me], recv1.at[me], recv_sem.at[0]).start()
+    to_sibling = [
+        send(seq_pair.at[core], seq_pair.at[core], 5, sibling),
+        send(cot_pair.at[core], cot_pair.at[core], 6, sibling),
+    ]
+
+    for n in range(5, 10):
+        loads[n].wait()
     twr = tw_ref[:, 0:lanes]
     twi = tw_ref[:, lanes : 2 * lanes]
-    first = (t1h[...], t1l[...])
-    second = (t2h[...], t2l[...])
-    second_back = (u2h[...], u2l[...])
-    first_back = (u1h[...], u1l[...])
+    first = tab_ref[0:256, :]
+    second = (tab_ref[256:512, :], tab_ref[512:768, :])
+    second_back = (tab_ref[768:1024, :], tab_ref[1024:1280, :])
+    first_back = (tab_ref[1280:1408, :], tab_ref[1408:1536, :])
 
     def forward(signals):
-        data = halves(jnp.concatenate(signals, axis=1))
-        mid = dot3(first, data)
+        high, low = halves(jnp.concatenate(signals, axis=1))
+        mid = dot(first, jnp.concatenate([high, high], axis=0)) + dot(first[:, 0:lanes], low)
         rows = []
         for i in range(len(signals)):
             re = mid[0:blocks, i * lanes : (i + 1) * lanes]
@@ -229,7 +285,7 @@
     stage_b[...] = recv1[...].astype(f32).reshape(count * 8, lanes)
 
     def tap(s, c, k):
-        return taps_ref[pl.ds(width * s + 2 * me + c, 1), k : k + 1]
+        return taps_ref[k, width * s + 2 * me + c]
 
     shifted = []
     streams = []
@@ -276,8 +332,8 @@
             stage_a[pl.ds(2 * s + c, count, stride=8), :] = total
     for c in range(2):
         stage_a[pl.ds(6 + c, count, stride=8), :] = gate_two[c] * second_mix[c]
-    send2[...] = stage_a[...].reshape(count, 8, lanes).astype(bf16)
-    exchange(lambda peer: send2.at[peer], recv2, 1)
+    send2[...] = stage_a[...].reshape(chips, 2, 8, lanes).astype(bf16)
+    exchange(lambda peer_chip: send2.at[peer_chip], recv2.at[chip], 1)
 
     line = jnp.zeros((1, lanes), f32)
     short_lane = lax.broadcasted_iota(jnp.int32, (1, lanes), 1)
@@ -287,7 +343,7 @@
             part = jnp.sum(part, axis=1, keepdims=True)
             line = jnp.where(short_lane == 3 * j + k, part * scale, line)
     short_slab[...] = line
-    exchange(lambda peer: short_slab, recv_short, 2)
+    exchange(lambda peer_chip: short_slab, shorts.at[core, chip], 2)
     grads = backward(
         [conj_times(spec_value[c], spec_gfm[c]) for c in range(2)]
         + [conj_times(spec_fo[c], spec_gsm[c]) for c in range(2)]
@@ -295,60 +351,128 @@
     for c in range(2):
         gf1_ref[pl.ds(c, count, stride=2), :] = grads[c] * scale
         gf2_ref[pl.ds(c, count, stride=2), :] = grads[2 + c] * scale
+    stores = [
+        pltpu.make_async_copy(gf1_ref, gf1_out, out_sem.at[0]),
+        pltpu.make_async_copy(gf2_ref, gf2_out, out_sem.at[1]),
+    ]
+    for store in stores:
+        store.start()
+    for copy in to_sibling:
+        copy.wait()
+    seq_both = jnp.concatenate([seq_pair[0], seq_pair[1]], axis=1)
+    cot_both = jnp.concatenate([cot_pair[0], cot_pair[1]], axis=1)
 
     arrived(recv2, 1)
-    stage_b[...] = recv2[...].astype(f32).reshape(count * 8, lanes)
-    rows = stage_b[...].astype(bf16)
-    with_seq = dot_nt(rows, seq_scr[...])
-    with_cot = dot_nt(rows, cot_ref[...])
-    kind = lax.broadcasted_iota(jnp.int32, (count * 8, 256), 0) % 8
+    rows_to_sibling = send(recv2.at[:, 1 - core], other_rows, 7, sibling)
+    block_rows = [recv2[:, k].astype(f32).reshape(chips * 8, lanes) for k in range(2)]
+    rows = jnp.concatenate([r.astype(bf16) for r in block_rows], axis=1)
+    with_seq = dot_nt(rows, seq_both)
+    with_cot = dot_nt(rows, cot_both)
+    kind = lax.broadcasted_iota(jnp.int32, (chips * 8, 256), 0) % 8
     partial = jnp.where(kind < 6, with_seq, with_cot) * scale
-    send3[...] = partial.reshape(count, 8, 256).astype(bf16)
-    exchange(lambda peer: send3.at[peer], recv3, 3)
-
-    for s in range(3):
-        for c in range(2):
-            stage_a[pl.ds(width * s + c, count, stride=2), :] = stage_b[
-                pl.ds(2 * s + c, count, stride=8), :
-            ]
+    send3[...] = partial.reshape(chips, 8, 256).astype(bf16)
+    exchange(lambda peer_chip: send3.at[peer_chip], recv3.at[chip], 3)
+
+    rows_to_sibling.wait()
+    own = jnp.where(core == 0, block_rows[0], block_rows[1])
+    other = other_rows[...].astype(f32).reshape(chips * 8, lanes)
+    stage_b[0 : chips * 8, :] = jnp.where(core == 0, own, other)
+    stage_b[chips * 8 : count * 8, :] = jnp.where(core == 0, other, own)
+    for half in range(2):
+        for s in range(3):
+            for c in range(2):
+                stage_a[pl.ds(width * s + 2 * half + c, chips, stride=4), :] = stage_b[
+                    pl.ds(chips * 8 * half + 2 * s + c, chips, stride=8), :
+                ]
     grad_projected = stage_a[0 : 3 * width, :].astype(bf16)
     grad_seq = dot_tn(win_ref[...], grad_projected).astype(bf16)
     gfeat_ref[...] = dot_nt(grad_seq, pick).astype(bf16)
+    stores.append(pltpu.make_async_copy(gfeat_ref, gfeat_out, out_sem.at[2]))
+    stores[2].start()
+    arrived(shorts.at[core], 2)
+    shorts_to_sibling = send(shorts.at[core], shorts.at[core], 9, sibling)
 
     arrived(recv3, 3)
     slab[...] = jnp.sum(recv3[...].astype(f32), axis=0).astype(bf16)
-    exchange(lambda peer: slab, recv4, 4)
-    arrived(recv_short, 2)
-    gathered = recv_short[...].reshape(count, lanes)
+    exchange(lambda peer_chip: slab, sums.at[core, chip], 4)
+    shorts_to_sibling.wait()
+    stores.append(pltpu.make_async_copy(shorts, short_out, out_sem.at[3]))
+    stores[3].start()
+    sent(send1, 0)
+    sent(send2, 1)
+    sent(shorts.at[0], 2)
+    sent(send3, 3)
+    arrived(sums.at[core], 4)
+    sums_to_sibling = send(sums.at[core], sums.at[core], 8, sibling)
+    sums_to_sibling.wait()
+    sent(sums.at[0], 4)
+    stores.append(pltpu.make_async_copy(sums, sums_out, out_sem.at[4]))
+    stores[4].start()
+    for store in stores:
+        store.wait()
+
+
+def finish_kernel(
+    count,
+    sums_ref,
+    short_ref,
+    gfeat_in,
+    gf1_in,
+    gf2_in,
+    gfeat_ref,
+    gwin_ref,
+    gwout_ref,
+    gshort_ref,
+    gf1_ref,
+    gf2_ref,
+    stage_a,
+    stage_b,
+):
+    chips = count // 2
+    lanes = 128
+    width = 2 * count
+    gfeat_ref[...] = gfeat_in[...]
+    gf1_ref[...] = gf1_in[...]
+    gf2_ref[...] = gf2_in[...]
+    for half in range(2):
+        stage_a[pl.ds(half, chips, stride=2), :] = short_ref[half].reshape(chips, lanes)
+    by_owner = stage_a[0:count, :]
+    owner = lax.broadcasted_iota(jnp.int32, (count, width), 0)
+    column = lax.broadcasted_iota(jnp.int32, (count, width), 1)
+    spread = [
+        lax.dot_general(
+            by_owner,
+            jnp.where(column == 2 * owner + c, 1.0, 0.0),
+            (((0,), (0,)), ((), ())),
+            preferred_element_type=f32,
+            precision=lax.Precision.HIGHEST,
+        )
+        for c in range(2)
+    ]
     for s in range(3):
-        for c in range(2):
-            j = 2 * s + c
-            gshort_ref[pl.ds(width * s + c, count, stride=2), :] = gathered[:, 3 * j : 3 * j + 3]
-    arrived(recv4, 4)
-    total = recv4[...].astype(f32).reshape(count * 8, 256)
+        gshort_ref[:, width * s : width * (s + 1)] = (
+            spread[0][6 * s : 6 * s + 3, :] + spread[1][6 * s + 3 : 6 * s + 6, :]
+        )
+    total = sums_ref[...].astype(f32).reshape(count * 8, 256)
     for h in range(2):
         stage_b[...] = total[:, h * lanes : (h + 1) * lanes]
-        for s in range(4):
-            for c in range(2):
-                stage_a[pl.ds(width * s + c, count, stride=2), :] = stage_b[
-                    pl.ds(2 * s + c, count, stride=8), :
-                ]
+        for half in range(2):
+            for s in range(4):
+                for c in range(2):
+                    stage_a[pl.ds(width * s + 2 * half + c, chips, stride=4), :] = stage_b[
+                        pl.ds(chips * 8 * half + 2 * s + c, chips, stride=8), :
+                    ]
         gwin_ref[:, h * lanes : (h + 1) * lanes] = stage_a[0 : 3 * width, :]
         gwout_ref[h * lanes : (h + 1) * lanes, :] = stage_a[3 * width : 4 * width, :].T
 
-    sent(send1, 0)
-    sent(send2, 1)
-    sent(recv_short, 2)
-    sent(send3, 3)
-    sent(recv4, 4)
-
 
 def local(
-    count, fft_size, features, sink_order, cotangent, w_in, short_taps, w_out, filter_one, filter_two
+    count, features, sink_order, cotangent, w_in, short_taps, w_out, filter_one, filter_two
 ):
     width, lanes = features.shape
     length = filter_one.shape[1]
-    tables = [jnp.asarray(t) for t in transform_tables(count, lanes)]
+    chips = count // 2
+    tables, twiddle = (jnp.asarray(t) for t in transform_tables(count, lanes))
 
     def by_row(filt):
         return filt.reshape(2, count, lanes).transpose(1, 0, 2).reshape(2 * count, lanes)
@@ -356,58 +480,95 @@
     def by_channel(grad):
         return grad.reshape(count, 2, lanes).transpose(1, 0, 2).reshape(2, length)
 
+    anywhere = pl.BlockSpec(memory_space=pl.ANY)
     vmem = pl.BlockSpec(memory_space=pltpu.VMEM)
     shape = jax.ShapeDtypeStruct
-    out = pl.pallas_call(
-        functools.partial(kernel, count, fft_size),
+    grad_shapes = (
+        shape((width, lanes), bf16),
+        shape((width, lanes), f32),
+        shape((width, lanes), f32),
+    )
+    sums, shorts, gfeat, gf1, gf2 = pl.pallas_call(
+        functools.partial(kernel, count),
         out_shape=(
-            shape((width, lanes), bf16),
-            shape((3 * width, width), f32),
-            shape((width, width), f32),
-            shape((3 * width, 3), f32),
-            shape((width, lanes), f32),
-            shape((width, lanes), f32),
+            shape((2, chips, 8, width), bf16),
+            shape((2, chips, 1, lanes), f32),
+            *grad_shapes,
         ),
-        in_specs=[vmem] * 17,
-        out_specs=(vmem,) * 6,
+        in_specs=[anywhere] * 10,
+        out_specs=(anywhere,) * 5,
         scratch_shapes=[
+            pltpu.VMEM((width, lanes), bf16),
+            pltpu.VMEM((1, lanes), jnp.int32),
+            pltpu.VMEM((2, width, lanes), bf16),
+            pltpu.VMEM((3 * width, width), bf16),
+            pltpu.VMEM((width, width), bf16),
+            pltpu.SMEM((3, 3 * width), f32),
+            pltpu.VMEM((width, lanes), f32),
+            pltpu.VMEM((width, lanes), f32),
+            pltpu.VMEM(tables.shape, bf16),
+            pltpu.VMEM(twiddle.shape, f32),
+            pltpu.VMEM((width, lanes), bf16),
+            pltpu.VMEM((width, lanes), f32),
+            pltpu.VMEM((width, lanes), f32),
             pltpu.VMEM((8 * count, lanes), f32),
             pltpu.VMEM((8 * count, lanes), f32),
-            pltpu.VMEM((width, lanes), bf16),
+            pltpu.VMEM((2, width, lanes), bf16),
             pltpu.VMEM((count, 8, lanes), bf16),
             pltpu.VMEM((count, 8, lanes), bf16),
-            pltpu.VMEM((count, 8, lanes), bf16),
-            pltpu.VMEM((count, 8, lanes), bf16),
-            pltpu.VMEM((count, 8, width), bf16),
-            pltpu.VMEM((count, 8, width), bf16),
+            pltpu.VMEM((chips, 2, 8, lanes), bf16),
+            pltpu.VMEM((chips, 2, 8, lanes), bf16),
+            pltpu.VMEM((chips, 8, lanes), bf16),
+            pltpu.VMEM((chips, 8, width), bf16),
+            pltpu.VMEM((chips, 8, width), bf16),
             pltpu.VMEM((8, width), bf16),
-            pltpu.VMEM((count, 8, width), bf16),
+            pltpu.VMEM((2, chips, 8, width), bf16),
             pltpu.VMEM((1, lanes), f32),
-            pltpu.VMEM((count, 1, lanes), f32),
+            pltpu.VMEM((2, chips, 1, lanes), f32),
+            pltpu.SemaphoreType.DMA((10,)),
             pltpu.SemaphoreType.DMA((5,)),
-            pltpu.SemaphoreType.DMA((5,)),
+            pltpu.SemaphoreType.DMA((10,)),
+            pltpu.SemaphoreType.DMA((10,)),
         ],
         compiler_params=pltpu.CompilerParams(collective_id=0, has_side_effects=True),
+        name="hyena_backward",
     )(
         features,
         sink_order,
         cotangent,
         w_in,
-        short_taps,
         w_out,
+        short_taps.T,
         by_row(filter_one),
         by_row(filter_two),
-        *tables,
-    )
-    gfeat, gwin, gwout, gshort, gf1, gf2 = out
-    return gfeat, gwin, gwout, gshort, by_channel(gf1), by_channel(gf2)
+        tables,
+        twiddle,
+    )
+    gfeat, gwin, gwout, gshort, gf1, gf2 = pl.pallas_call(
+        functools.partial(finish_kernel, count),
+        out_shape=(
+            grad_shapes[0],
+            shape((3 * width, width), f32),
+            shape((width, width), f32),
+            shape((3, 3 * width), f32),
+            *grad_shapes[1:],
+        ),
+        in_specs=[vmem] * 5,
+        out_specs=(vmem,) * 6,
+        scratch_shapes=[
+            pltpu.VMEM((8 * count, lanes), f32),
+            pltpu.VMEM((8 * count, lanes), f32),
+        ],
+        name="row_order",
+    )(sums, shorts, gfeat, gf1, gf2)
+    return gfeat, gwin, gwout, gshort.T, by_channel(gf1), by_channel(gf2)
 
 
 def solution(mesh):
     count = mesh.shape["seq"] * mesh.shape["fft"]
     both = ("seq", "fft")
     return jax.shard_map(
-        functools.partial(local, count, mesh.shape["fft"]),
+        functools.partial(local, count),
         mesh=mesh,
         in_specs=(
             P(None, both),

time: 63.6 us -> 46 us (0.72)
  local copies, waits for them, and re-layouts: 8.76 us -> 0 us
  Pallas kernels: 53.9 us -> 45.2 us
    unnamed x15 -> x0, local copies, waits for them, and re-layouts: 8.76 us -> none
    pallas_call x1 -> x2, Pallas kernels: 53.9 us -> 45.2 us  [the longest x1 42.4 us: local(): pl.pallas_call(functools.partial(kernel, count), out_shape=(shape((2, chi...]
where the time goes in v2:
time: 46 us; the launch traced here: 45.8 us
  Pallas kernels  45.2 us (98%)
  between operations  0.64 us (1%)
    pallas_call x1, Pallas kernels, local(): pl.pallas_call(functools.partial(kernel, count), out_shape=(shape((2, chi...  42.4 us
    pallas_call x1, Pallas kernels, local(): pl.pallas_call(functools.partial(finish_kernel, count), out_shape=(grad_s...  2.82 us

profile of v2, /device:TPU:1, one launch (start us, length us, event | category | flops | bytes accessed | tf_op | source)
XLA Modules:
  0.0 45.8 jit_solution(728867248290159040)
XLA Ops:
  0.6 42.4 %hyena_backward.1 = (bf16[2,64,8,256]{3,2,1,0:T(8,128)(2,1)}, f32[2,64,1,128]{3,2,1,0:T(1,128)}, bf16[256,128]{1,0:T(8,128)(2,1)}, f32[256,128]{1,0:T(8,128)}, f32[256,128]{1,0:T(8,128)}) custom-call(bf16[256,128]{1,0:T(8,128)(2,1)} %feat_in.1, s32[1,128]{1,0:T(1,128)} %order_in.1, bf16[256,128]{1,0:T(8,128)(2,1)} %cot_in.1, bf16[768,256]{1,0:T(8,128)(2,1)} %win_in.1, ...), custom_call_target="tpu_custom_call" | custom-call | tf_op jit(solution)/shard_map/hyena_backward/pallas_call | solution.py:491
  43.0 2.8 %row_order.1 = (bf16[256,128]{1,0:T(8,128)(2,1)}, f32[768,256]{1,0:T(8,128)}, f32[256,256]{1,0:T(8,128)}, f32[3,768]{1,0:T(4,128)}, f32[256,128]{1,0:T(8,128)}, /*index=5*/f32[256,128]{1,0:T(8,128)}) custom-call(bf16[2,64,8,256]{3,2,1,0:T(8,128)(2,1)} %get-tuple-element.17.sums_ref, f32[2,64,1,128]{3,2,1,0:T(1,128)} %get-tuple-element.18.short_ref, ...), custom_call_target="tpu_custom_call" | custom-call | tf_op jit(solution)/shard_map/row_order/pallas_call | solution.py:547

commit v3 on v2

--- a/solution.py
+++ b/solution.py
@@ -14,11 +14,20 @@
 f32 = jnp.float32
 LOGICAL = pl.DeviceIdType.LOGICAL
 SIDE = 4
+FAR = 5
+
+
+def hops(step):
+    return sum(min(d, SIDE - d) for d in step)
 
 
 def chip_offsets():
     steps = [(a, b, c) for a in range(SIDE) for b in range(SIDE) for c in range(SIDE) if a + b + c]
-    return sorted(steps, key=lambda step: -sum(min(d, SIDE - d) for d in step))
+    return sorted(steps, key=lambda step: -hops(step))
+
+
+def plane_offsets():
+    return [step for step in chip_offsets() if step[0] == 0]
 
 
 def table_halves(table):
@@ -88,7 +97,7 @@
     gf2_out,
     feat_ref,
     order_ref,
-    cot_pair,
+    cot_line,
     win_ref,
     wout_ref,
     taps_ref,
@@ -101,12 +110,12 @@
     gf2_ref,
     stage_a,
     stage_b,
-    seq_pair,
+    seq_line,
     send1,
     recv1,
     send2,
     recv2,
-    other_rows,
+    rows_line,
     send3,
     recv3,
     slab,
@@ -117,6 +126,7 @@
     out_sem,
     send_sem,
     recv_sem,
+    ready_sem,
 ):
     blocks = count
     chips = count // 2
@@ -137,6 +147,14 @@
     me = 2 * chip + core
     sibling = 2 * chip + (1 - core)
     other_chips = [along_x[a] + along_y[b] + along_z[c] for a, b, c in chip_offsets()]
+    in_line = [(x + d) % SIDE % 2 * 2 + (x + d) % SIDE // 2 for d in range(SIDE)]
+    line_chips = [along_x[d] + along_y[0] + along_z[0] for d in range(SIDE)]
+    here = z * SIDE + y
+    plane = [
+        ((z + c) % SIDE * SIDE + (y + b) % SIDE, along_x[0] + along_y[b] + along_z[c])
+        for _, b, c in plane_offsets()
+    ]
+    mine = in_line[0]
 
     loads = [
         pltpu.make_async_copy(source, target, in_sem.at[n])
@@ -144,7 +162,7 @@
             (
                 (feat_in, feat_ref),
                 (order_in, order_ref),
-                (cot_in, cot_pair.at[core]),
+                (cot_in, cot_line.at[core, mine]),
                 (win_in, win_ref),
                 (wout_in, wout_ref),
                 (taps_in, taps_ref),
@@ -159,10 +177,9 @@
         load.start()
     barrier = pltpu.get_barrier_semaphore()
     for peer_chip in other_chips:
-        for c in range(2):
-            pl.semaphore_signal(
-                barrier, inc=1, device_id=2 * peer_chip + c, device_id_type=LOGICAL
-            )
+        pl.semaphore_signal(
+            barrier, inc=1, device_id=2 * peer_chip + core, device_id_type=LOGICAL
+        )
     pl.semaphore_signal(barrier, inc=1, device_id=sibling, device_id_type=LOGICAL)
 
     def send(source, target, phase, peer):
@@ -185,8 +202,12 @@
     def arrived(whole, phase):
         pltpu.make_async_copy(whole, whole, recv_sem.at[phase]).wait()
 
-    def sent(whole, phase):
-        part = whole.at[pl.ds(0, whole.shape[0] - 1)]
+    def plane_exchange(source, target, phase):
+        for place, peer_chip in plane:
+            send(source.at[place], target.at[here], phase, 2 * peer_chip + core)
+        pltpu.make_async_copy(source.at[here], target.at[here], recv_sem.at[phase]).start()
+
+    def sent(part, phase):
         pltpu.make_async_copy(part, part, send_sem.at[phase]).wait()
 
     for n in range(5):
@@ -196,9 +217,9 @@
         lax.broadcasted_iota(jnp.int32, (lanes, lanes), 0) == order, 1.0, 0.0
     ).astype(bf16)
     seq_input = dot(feat_ref[...], pick).astype(bf16)
-    seq_pair[core] = seq_input
+    seq_line[core, mine] = seq_input
     stage_a[0 : 3 * width, :] = dot(win_ref[...], seq_input)
-    stage_a[3 * width : 4 * width, :] = dot_tn(wout_ref[...], cot_pair[core])
+    stage_a[3 * width : 4 * width, :] = dot_tn(wout_ref[...], cot_line[core, mine])
     for s in range(4):
         for c in range(2):
             stage_b[pl.ds(2 * s + c, count, stride=8), :] = stage_a[
@@ -206,17 +227,15 @@
             ]
     send1[...] = stage_b[...].reshape(count, 8, lanes).astype(bf16)
 
-    pl.semaphore_wait(barrier, count - 1)
+    pl.semaphore_wait(barrier, chips)
+    pl.semaphore_signal(ready_sem, inc=1, device_id=sibling, device_id_type=LOGICAL)
+    pl.semaphore_wait(ready_sem, 1)
     for peer_chip in other_chips:
         for c in range(2):
             peer = 2 * peer_chip + c
             send(send1.at[peer], recv1.at[me], 0, peer)
     send(send1.at[sibling], recv1.at[me], 0, sibling)
     pltpu.make_async_copy(send1.at[me], recv1.at[me], recv_sem.at[0]).start()
-    to_sibling = [
-        send(seq_pair.at[core], seq_pair.at[core], 5, sibling),
-        send(cot_pair.at[core], cot_pair.at[core], 6, sibling),
-    ]
 
     for n in range(5, 10):
         loads[n].wait()
@@ -280,6 +299,11 @@
     ]
     spec_f = forward(filters)
     spec_f1, spec_f2 = spec_f[0:2], spec_f[2:4]
+
+    for d in (2, 1, 3):
+        own_seq, own_cot = seq_line.at[core, mine], cot_line.at[core, mine]
+        send(own_seq, own_seq, 5, 2 * line_chips[d] + core)
+        send(own_cot, own_cot, 6, 2 * line_chips[d] + core)
 
     arrived(recv1, 0)
     stage_b[...] = recv1[...].astype(f32).reshape(count * 8, lanes)
@@ -332,8 +356,19 @@
             stage_a[pl.ds(2 * s + c, count, stride=8), :] = total
     for c in range(2):
         stage_a[pl.ds(6 + c, count, stride=8), :] = gate_two[c] * second_mix[c]
-    send2[...] = stage_a[...].reshape(chips, 2, 8, lanes).astype(bf16)
-    exchange(lambda peer_chip: send2.at[peer_chip], recv2.at[chip], 1)
+    outgoing = stage_a[...].reshape(2, SIDE * SIDE, 2, 2, 8, lanes)
+    for k in range(2):
+        for low in range(2):
+            for high in range(2):
+                send2[:, 4 * k + 2 * low + high] = outgoing[low, :, high, k].astype(bf16)
+    plane_exchange(send2, recv2, 1)
+    line_rest = pl.ds(0, SIDE - 1)
+    arrived(seq_line.at[0, line_rest], 5)
+    arrived(cot_line.at[0, line_rest], 6)
+    line_to_sibling = [
+        send(seq_line.at[core], seq_line.at[core], 11, sibling),
+        send(cot_line.at[core], cot_line.at[core], 12, sibling),
+    ]
 
     line = jnp.zeros((1, lanes), f32)
     short_lane = lax.broadcasted_iota(jnp.int32, (1, lanes), 1)
@@ -357,55 +392,86 @@
     ]
     for store in stores:
         store.start()
-    for copy in to_sibling:
+    for copy in line_to_sibling:
         copy.wait()
-    seq_both = jnp.concatenate([seq_pair[0], seq_pair[1]], axis=1)
-    cot_both = jnp.concatenate([cot_pair[0], cot_pair[1]], axis=1)
+    line_blocks = [(k, p) for k in range(2) for p in range(SIDE)]
+    seq_all = jnp.concatenate([seq_line[k, p] for k, p in line_blocks], axis=1)
+    cot_all = jnp.concatenate([cot_line[k, p] for k, p in line_blocks], axis=1)
 
     arrived(recv2, 1)
-    rows_to_sibling = send(recv2.at[:, 1 - core], other_rows, 7, sibling)
-    block_rows = [recv2[:, k].astype(f32).reshape(chips * 8, lanes) for k in range(2)]
-    rows = jnp.concatenate([r.astype(bf16) for r in block_rows], axis=1)
-    with_seq = dot_nt(rows, seq_both)
-    with_cot = dot_nt(rows, cot_both)
-    kind = lax.broadcasted_iota(jnp.int32, (chips * 8, 256), 0) % 8
+    rows = jnp.concatenate(
+        [recv2[:, n].astype(f32).reshape(count, lanes).astype(bf16) for n in range(2 * SIDE)],
+        axis=1,
+    )
+    with_seq = dot_nt(rows, seq_all)
+    with_cot = dot_nt(rows, cot_all)
+    kind = lax.broadcasted_iota(jnp.int32, (count, 256), 0) % 8
     partial = jnp.where(kind < 6, with_seq, with_cot) * scale
-    send3[...] = partial.reshape(chips, 8, 256).astype(bf16)
-    exchange(lambda peer_chip: send3.at[peer_chip], recv3.at[chip], 3)
-
-    rows_to_sibling.wait()
-    own = jnp.where(core == 0, block_rows[0], block_rows[1])
-    other = other_rows[...].astype(f32).reshape(chips * 8, lanes)
-    stage_b[0 : chips * 8, :] = jnp.where(core == 0, own, other)
-    stage_b[chips * 8 : count * 8, :] = jnp.where(core == 0, other, own)
-    for half in range(2):
-        for s in range(3):
+    send3[...] = partial.reshape(SIDE * SIDE, 8, 256).astype(bf16)
+    plane_exchange(send3, recv3, 3)
+    own_rows = rows_line.at[mine, core]
+    for d in (2, 1, 3):
+        for c in range(2):
+            send(recv2.at[:, SIDE * c + in_line[d]], own_rows, 7, 2 * line_chips[d] + c)
+    send(recv2.at[:, SIDE * (1 - core) + mine], own_rows, 7, sibling)
+    pltpu.make_async_copy(recv2.at[:, SIDE * core + mine], own_rows, recv_sem.at[7]).start()
+    arrived(shorts.at[core], 2)
+    shorts_to_sibling = send(shorts.at[core], shorts.at[core], 9, sibling)
+
+    arrived(recv3, 3)
+    slab[...] = jnp.sum(recv3[...].astype(f32), axis=0).astype(bf16)
+    near = []
+    far = 0
+    for step, peer_chip in zip(chip_offsets(), other_chips):
+        if hops(step) >= FAR:
             for c in range(2):
-                stage_a[pl.ds(width * s + 2 * half + c, chips, stride=4), :] = stage_b[
-                    pl.ds(chips * 8 * half + 2 * s + c, chips, stride=8), :
-                ]
+                send(slab, sums.at[core, chip], 10, 2 * peer_chip + c)
+            far += 2
+        else:
+            send(slab, sums.at[core, chip], 4, 2 * peer_chip + core)
+            near.append(peer_chip)
+    pltpu.make_async_copy(slab, sums.at[core, chip], recv_sem.at[4]).start()
+
+    arrived(rows_line, 7)
+    by_place = [
+        jnp.stack([rows_line[k, p].astype(f32) for p in range(2)], axis=1) for k in range(SIDE)
+    ]
+    stage_b[...] = jnp.stack(
+        [jnp.stack([by_place[2 * low + high] for high in range(2)], axis=1) for low in range(2)],
+        axis=0,
+    ).reshape(count * 8, lanes)
+    for s in range(3):
+        for c in range(2):
+            stage_a[pl.ds(width * s + c, count, stride=2), :] = stage_b[
+                pl.ds(2 * s + c, count, stride=8), :
+            ]
     grad_projected = stage_a[0 : 3 * width, :].astype(bf16)
     grad_seq = dot_tn(win_ref[...], grad_projected).astype(bf16)
     gfeat_ref[...] = dot_nt(grad_seq, pick).astype(bf16)
     stores.append(pltpu.make_async_copy(gfeat_ref, gfeat_out, out_sem.at[2]))
     stores[2].start()
-    arrived(shorts.at[core], 2)
-    shorts_to_sibling = send(shorts.at[core], shorts.at[core], 9, sibling)
-
-    arrived(recv3, 3)
-    slab[...] = jnp.sum(recv3[...].astype(f32), axis=0).astype(bf16)
-    exchange(lambda peer_chip: slab, sums.at[core, chip], 4)
     shorts_to_sibling.wait()
     stores.append(pltpu.make_async_copy(shorts, short_out, out_sem.at[3]))
     stores[3].start()
-    sent(send1, 0)
-    sent(send2, 1)
-    sent(shorts.at[0], 2)
-    sent(send3, 3)
-    arrived(sums.at[core], 4)
-    sums_to_sibling = send(sums.at[core], sums.at[core], 8, sibling)
-    sums_to_sibling.wait()
-    sent(sums.at[0], 4)
+
+    near_slots = sums.at[0, pl.ds(0, len(near) + 1)]
+    far_slots = sums.at[0, pl.ds(0, far)]
+    arrived(near_slots, 4)
+    for peer_chip in near + [chip]:
+        send(sums.at[core, peer_chip], sums.at[core, peer_chip], 8, sibling)
+    sent(send1.at[pl.ds(0, count - 1)], 0)
+    sent(seq_line.at[0, line_rest], 5)
+    sent(cot_line.at[0, line_rest], 6)
+    sent(shorts.at[0, pl.ds(0, chips - 1)], 2)
+    place_rest = pl.ds(0, SIDE * SIDE - 1)
+    sent(send2.at[place_rest], 1)
+    sent(send3.at[place_rest], 3)
+    sent(recv1.at[pl.ds(0, count - SIDE * SIDE)], 7)
+    arrived(far_slots, 10)
+    arrived(near_slots, 8)
+    sent(sums.at[0, pl.ds(0, len(near))], 4)
+    sent(far_slots, 10)
+    sent(near_slots, 8)
     stores.append(pltpu.make_async_copy(sums, sums_out, out_sem.at[4]))
     stores[4].start()
     for store in stores:
@@ -500,7 +566,7 @@
         scratch_shapes=[
             pltpu.VMEM((width, lanes), bf16),
             pltpu.VMEM((1, lanes), jnp.int32),
-            pltpu.VMEM((2, width, lanes), bf16),
+            pltpu.VMEM((2, SIDE, width, lanes), bf16),
             pltpu.VMEM((3 * width, width), bf16),
             pltpu.VMEM((width, width), bf16),
             pltpu.SMEM((3, 3 * width), f32),
@@ -513,22 +579,23 @@
             pltpu.VMEM((width, lanes), f32),
             pltpu.VMEM((8 * count, lanes), f32),
             pltpu.VMEM((8 * count, lanes), f32),
-            pltpu.VMEM((2, width, lanes), bf16),
+            pltpu.VMEM((2, SIDE, width, lanes), bf16),
             pltpu.VMEM((count, 8, lanes), bf16),
             pltpu.VMEM((count, 8, lanes), bf16),
-            pltpu.VMEM((chips, 2, 8, lanes), bf16),
-            pltpu.VMEM((chips, 2, 8, lanes), bf16),
-            pltpu.VMEM((chips, 8, lanes), bf16),
-            pltpu.VMEM((chips, 8, width), bf16),
-            pltpu.VMEM((chips, 8, width), bf16),
+            pltpu.VMEM((SIDE * SIDE, 2 * SIDE, 8, lanes), bf16),
+            pltpu.VMEM((SIDE * SIDE, 2 * SIDE, 8, lanes), bf16),
+            pltpu.VMEM((SIDE, 2, SIDE * SIDE, 8, lanes), bf16),
+            pltpu.VMEM((SIDE * SIDE, 8, width), bf16),
+            pltpu.VMEM((SIDE * SIDE, 8, width), bf16),
             pltpu.VMEM((8, width), bf16),
             pltpu.VMEM((2, chips, 8, width), bf16),
             pltpu.VMEM((1, lanes), f32),
             pltpu.VMEM((2, chips, 1, lanes), f32),
             pltpu.SemaphoreType.DMA((10,)),
             pltpu.SemaphoreType.DMA((5,)),
-            pltpu.SemaphoreType.DMA((10,)),
-            pltpu.SemaphoreType.DMA((10,)),
+            pltpu.SemaphoreType.DMA((13,)),
+            pltpu.SemaphoreType.DMA((13,)),
+            pltpu.SemaphoreType.REGULAR,
         ],
         compiler_params=pltpu.CompilerParams(collective_id=0, has_side_effects=True),
         name="hyena_backward",

time: 46 us -> 43.8 us (0.952)
  Pallas kernels: 45.2 us -> 43 us
    pallas_call x1, Pallas kernels: 42.4 us -> 40.2 us  [local(): pl.pallas_call(functools.partial(kernel, count), out_shape=(shape((2, chi...]
where the time goes in v3:
time: 43.8 us; the launch traced here: 43.7 us
  Pallas kernels  43 us (98%)
  between operations  0.64 us (1%)
    pallas_call x1, Pallas kernels, local(): pl.pallas_call(functools.partial(kernel, count), out_shape=(shape((2, chi...  40.2 us
    pallas_call x1, Pallas kernels, local(): pl.pallas_call(functools.partial(finish_kernel, count), out_shape=(grad_s...  2.82 us

profile of v3, /device:TPU:1, one launch (start us, length us, event | category | flops | bytes accessed | tf_op | source)
XLA Modules:
  0.0 43.7 jit_solution(7820359116510895929)
XLA Ops:
  0.6 40.2 %hyena_backward.1 = (bf16[2,64,8,256]{3,2,1,0:T(8,128)(2,1)}, f32[2,64,1,128]{3,2,1,0:T(1,128)}, bf16[256,128]{1,0:T(8,128)(2,1)}, f32[256,128]{1,0:T(8,128)}, f32[256,128]{1,0:T(8,128)}) custom-call(bf16[256,128]{1,0:T(8,128)(2,1)} %feat_in.1, s32[1,128]{1,0:T(1,128)} %order_in.1, bf16[256,128]{1,0:T(8,128)(2,1)} %cot_in.1, bf16[768,256]{1,0:T(8,128)(2,1)} %win_in.1, ...), custom_call_target="tpu_custom_call" | custom-call | tf_op jit(solution)/shard_map/hyena_backward/pallas_call | solution.py:557
  40.8 2.8 %row_order.1 = (bf16[256,128]{1,0:T(8,128)(2,1)}, f32[768,256]{1,0:T(8,128)}, f32[256,256]{1,0:T(8,128)}, f32[3,768]{1,0:T(4,128)}, f32[256,128]{1,0:T(8,128)}, /*index=5*/f32[256,128]{1,0:T(8,128)}) custom-call(bf16[2,64,8,256]{3,2,1,0:T(8,128)(2,1)} %get-tuple-element.17.sums_ref, f32[2,64,1,128]{3,2,1,0:T(1,128)} %get-tuple-element.18.short_ref, ...), custom_call_target="tpu_custom_call" | custom-call | tf_op jit(solution)/shard_map/row_order/pallas_call | solution.py:614

commit v4 on v3

--- a/solution.py
+++ b/solution.py
@@ -14,7 +14,7 @@
 f32 = jnp.float32
 LOGICAL = pl.DeviceIdType.LOGICAL
 SIDE = 4
-FAR = 5
+VIA_SIBLING = (3, 4)
 
 
 def hops(step):
@@ -90,7 +90,7 @@
     filt2_in,
     tab_in,
     tw_in,
-    sums_out,
+    sums,
     short_out,
     gfeat_out,
     gf1_out,
@@ -108,6 +108,7 @@
     gfeat_ref,
     gf1_ref,
     gf2_ref,
+    gshort_ref,
     stage_a,
     stage_b,
     seq_line,
@@ -119,7 +120,6 @@
     send3,
     recv3,
     slab,
-    sums,
     short_slab,
     shorts,
     in_sem,
@@ -156,6 +156,12 @@
     ]
     mine = in_line[0]
 
+    barrier = pltpu.get_barrier_semaphore()
+    for peer_chip in other_chips:
+        pl.semaphore_signal(
+            barrier, inc=1, device_id=2 * peer_chip + core, device_id_type=LOGICAL
+        )
+    pl.semaphore_signal(barrier, inc=1, device_id=sibling, device_id_type=LOGICAL)
     loads = [
         pltpu.make_async_copy(source, target, in_sem.at[n])
         for n, (source, target) in enumerate(
@@ -175,12 +181,6 @@
     ]
     for load in loads:
         load.start()
-    barrier = pltpu.get_barrier_semaphore()
-    for peer_chip in other_chips:
-        pl.semaphore_signal(
-            barrier, inc=1, device_id=2 * peer_chip + core, device_id_type=LOGICAL
-        )
-    pl.semaphore_signal(barrier, inc=1, device_id=sibling, device_id_type=LOGICAL)
 
     def send(source, target, phase, peer):
         copy = pltpu.make_async_remote_copy(
@@ -420,17 +420,22 @@
 
     arrived(recv3, 3)
     slab[...] = jnp.sum(recv3[...].astype(f32), axis=0).astype(bf16)
-    near = []
-    far = 0
-    for step, peer_chip in zip(chip_offsets(), other_chips):
-        if hops(step) >= FAR:
+    steps = sorted(
+        zip(chip_offsets(), other_chips), key=lambda item: hops(item[0]) not in VIA_SIBLING
+    )
+    relayed = []
+    direct = 0
+    own_sums = sums.at[core, chip]
+    for step, peer_chip in steps:
+        if hops(step) in VIA_SIBLING:
+            send(slab, own_sums, 4, 2 * peer_chip + core)
+            relayed.append(peer_chip)
+        else:
             for c in range(2):
-                send(slab, sums.at[core, chip], 10, 2 * peer_chip + c)
-            far += 2
-        else:
-            send(slab, sums.at[core, chip], 4, 2 * peer_chip + core)
-            near.append(peer_chip)
-    pltpu.make_async_copy(slab, sums.at[core, chip], recv_sem.at[4]).start()
+                send(slab, own_sums, 10, 2 * peer_chip + c)
+            direct += 2
+    send(slab, own_sums, 10, sibling)
+    pltpu.make_async_copy(slab, own_sums, recv_sem.at[10]).start()
 
     arrived(rows_line, 7)
     by_place = [
@@ -451,57 +456,8 @@
     stores.append(pltpu.make_async_copy(gfeat_ref, gfeat_out, out_sem.at[2]))
     stores[2].start()
     shorts_to_sibling.wait()
-    stores.append(pltpu.make_async_copy(shorts, short_out, out_sem.at[3]))
-    stores[3].start()
-
-    near_slots = sums.at[0, pl.ds(0, len(near) + 1)]
-    far_slots = sums.at[0, pl.ds(0, far)]
-    arrived(near_slots, 4)
-    for peer_chip in near + [chip]:
-        send(sums.at[core, peer_chip], sums.at[core, peer_chip], 8, sibling)
-    sent(send1.at[pl.ds(0, count - 1)], 0)
-    sent(seq_line.at[0, line_rest], 5)
-    sent(cot_line.at[0, line_rest], 6)
-    sent(shorts.at[0, pl.ds(0, chips - 1)], 2)
-    place_rest = pl.ds(0, SIDE * SIDE - 1)
-    sent(send2.at[place_rest], 1)
-    sent(send3.at[place_rest], 3)
-    sent(recv1.at[pl.ds(0, count - SIDE * SIDE)], 7)
-    arrived(far_slots, 10)
-    arrived(near_slots, 8)
-    sent(sums.at[0, pl.ds(0, len(near))], 4)
-    sent(far_slots, 10)
-    sent(near_slots, 8)
-    stores.append(pltpu.make_async_copy(sums, sums_out, out_sem.at[4]))
-    stores[4].start()
-    for store in stores:
-        store.wait()
-
-
-def finish_kernel(
-    count,
-    sums_ref,
-    short_ref,
-    gfeat_in,
-    gf1_in,
-    gf2_in,
-    gfeat_ref,
-    gwin_ref,
-    gwout_ref,
-    gshort_ref,
-    gf1_ref,
-    gf2_ref,
-    stage_a,
-    stage_b,
-):
-    chips = count // 2
-    lanes = 128
-    width = 2 * count
-    gfeat_ref[...] = gfeat_in[...]
-    gf1_ref[...] = gf1_in[...]
-    gf2_ref[...] = gf2_in[...]
     for half in range(2):
-        stage_a[pl.ds(half, chips, stride=2), :] = short_ref[half].reshape(chips, lanes)
+        stage_a[pl.ds(half, chips, stride=2), :] = shorts[half].reshape(chips, lanes)
     by_owner = stage_a[0:count, :]
     owner = lax.broadcasted_iota(jnp.int32, (count, width), 0)
     column = lax.broadcasted_iota(jnp.int32, (count, width), 1)
@@ -519,17 +475,98 @@
         gshort_ref[:, width * s : width * (s + 1)] = (
             spread[0][6 * s : 6 * s + 3, :] + spread[1][6 * s + 3 : 6 * s + 6, :]
         )
-    total = sums_ref[...].astype(f32).reshape(count * 8, 256)
+    stores.append(pltpu.make_async_copy(gshort_ref, short_out, out_sem.at[3]))
+    stores[3].start()
+
+    relayed_slots = sums.at[0, pl.ds(0, len(relayed))]
+    arrived(relayed_slots, 4)
+    for peer_chip in relayed:
+        send(sums.at[core, peer_chip], sums.at[core, peer_chip], 8, sibling)
+    sent(send1.at[pl.ds(0, count - 1)], 0)
+    sent(seq_line.at[0, line_rest], 5)
+    sent(cot_line.at[0, line_rest], 6)
+    sent(shorts.at[0, pl.ds(0, chips - 1)], 2)
+    place_rest = pl.ds(0, SIDE * SIDE - 1)
+    sent(send2.at[place_rest], 1)
+    sent(send3.at[place_rest], 3)
+    sent(recv1.at[pl.ds(0, count - SIDE * SIDE)], 7)
+    arrived(sums.at[0, pl.ds(0, direct + 2)], 10)
+    arrived(relayed_slots, 8)
+    sent(relayed_slots, 4)
+    sent(sums.at[0, pl.ds(0, direct + 1)], 10)
+    sent(relayed_slots, 8)
+    for store in stores:
+        store.wait()
+
+
+def finish_kernel(
+    count,
+    sums_in,
+    short_in,
+    gfeat_in,
+    gf1_in,
+    gf2_in,
+    gfeat_out,
+    gwin_out,
+    gwout_out,
+    gshort_out,
+    gf1_out,
+    gf2_out,
+    sums_ref,
+    gfeat_ref,
+    gf1_ref,
+    gf2_ref,
+    gwout_ref,
+    gshort_ref,
+    ordered,
+    stage,
+    in_sem,
+    out_sem,
+):
+    chips = count // 2
+    lanes = 128
+    width = 2 * count
+    loads = [
+        pltpu.make_async_copy(source, target, in_sem.at[n])
+        for n, (source, target) in enumerate(
+            (
+                (sums_in, sums_ref),
+                (short_in, gshort_ref),
+                (gf1_in, gf1_ref),
+                (gf2_in, gf2_ref),
+                (gfeat_in, gfeat_ref),
+            )
+        )
+    ]
+    for load in loads:
+        load.start()
+    stores = []
+
+    def store(source, target):
+        copy = pltpu.make_async_copy(source, target, out_sem.at[len(stores)])
+        copy.start()
+        stores.append(copy)
+
+    loads[0].wait()
     for h in range(2):
-        stage_b[...] = total[:, h * lanes : (h + 1) * lanes]
+        part = pl.ds(h * lanes, lanes)
+        stage[...] = sums_ref[:, :, :, part].astype(f32).reshape(count * 8, lanes)
         for half in range(2):
             for s in range(4):
                 for c in range(2):
-                    stage_a[pl.ds(width * s + 2 * half + c, chips, stride=4), :] = stage_b[
+                    ordered[h, pl.ds(width * s + 2 * half + c, chips, stride=4), :] = stage[
                         pl.ds(chips * 8 * half + 2 * s + c, chips, stride=8), :
                     ]
-        gwin_ref[:, h * lanes : (h + 1) * lanes] = stage_a[0 : 3 * width, :]
-        gwout_ref[h * lanes : (h + 1) * lanes, :] = stage_a[3 * width : 4 * width, :].T
+        store(ordered.at[h, pl.ds(0, 3 * width)], gwin_out.at[:, part])
+        gwout_ref[part, :] = ordered[h, 3 * width : 4 * width, :].T
+        store(gwout_ref.at[part], gwout_out.at[part])
+    for n, (ref, target) in enumerate(((gf1_ref, gf1_out), (gf2_ref, gf2_out), (gfeat_ref, gfeat_out))):
+        loads[2 + n].wait()
+        store(ref, target)
+    loads[1].wait()
+    store(gshort_ref, gshort_out)
+    for copy in stores:
+        copy.wait()
 
 
 def local(
@@ -547,7 +584,6 @@
         return grad.reshape(count, 2, lanes).transpose(1, 0, 2).reshape(2, length)
 
     anywhere = pl.BlockSpec(memory_space=pl.ANY)
-    vmem = pl.BlockSpec(memory_space=pltpu.VMEM)
     shape = jax.ShapeDtypeStruct
     grad_shapes = (
         shape((width, lanes), bf16),
@@ -558,7 +594,7 @@
         functools.partial(kernel, count),
         out_shape=(
             shape((2, chips, 8, width), bf16),
-            shape((2, chips, 1, lanes), f32),
+            shape((3, 3 * width), f32),
             *grad_shapes,
         ),
         in_specs=[anywhere] * 10,
@@ -577,6 +613,7 @@
             pltpu.VMEM((width, lanes), bf16),
             pltpu.VMEM((width, lanes), f32),
             pltpu.VMEM((width, lanes), f32),
+            pltpu.VMEM((3, 3 * width), f32),
             pltpu.VMEM((8 * count, lanes), f32),
             pltpu.VMEM((8 * count, lanes), f32),
             pltpu.VMEM((2, SIDE, width, lanes), bf16),
@@ -588,7 +625,6 @@
             pltpu.VMEM((SIDE * SIDE, 8, width), bf16),
             pltpu.VMEM((SIDE * SIDE, 8, width), bf16),
             pltpu.VMEM((8, width), bf16),
-            pltpu.VMEM((2, chips, 8, width), bf16),
             pltpu.VMEM((1, lanes), f32),
             pltpu.VMEM((2, chips, 1, lanes), f32),
             pltpu.SemaphoreType.DMA((10,)),
@@ -620,11 +656,19 @@
             shape((3, 3 * width), f32),
             *grad_shapes[1:],
         ),
-        in_specs=[vmem] * 5,
-        out_specs=(vmem,) * 6,
+        in_specs=[anywhere] * 5,
+        out_specs=(anywhere,) * 6,
         scratch_shapes=[
+            pltpu.VMEM((2, chips, 8, width), bf16),
+            pltpu.VMEM((width, lanes), bf16),
+            pltpu.VMEM((width, lanes), f32),
+            pltpu.VMEM((width, lanes), f32),
+            pltpu.VMEM((width, width), f32),
+            pltpu.VMEM((3, 3 * width), f32),
+            pltpu.VMEM((2, 8 * count, lanes), f32),
             pltpu.VMEM((8 * count, lanes), f32),
-            pltpu.VMEM((8 * count, lanes), f32),
+            pltpu.SemaphoreType.DMA((5,)),
+            pltpu.SemaphoreType.DMA((8,)),
         ],
         name="row_order",
     )(sums, shorts, gfeat, gf1, gf2)

time: 43.8 us -> 42.7 us (0.975)
  Pallas kernels: 43 us -> 41.9 us
    pallas_call x1, Pallas kernels: 40.2 us -> 39.5 us  [local(): pl.pallas_call(functools.partial(kernel, count), out_shape=(shape((2, chi...]
where the time goes in v4:
time: 42.7 us; the launch traced here: 42.5 us
  Pallas kernels  41.9 us (98%)
  between operations  0.64 us (1%)
    pallas_call x1, Pallas kernels, local(): pl.pallas_call(functools.partial(kernel, count), out_shape=(shape((2, chi...  39.5 us
    pallas_call x1, Pallas kernels, local(): pl.pallas_call(functools.partial(finish_kernel, count), out_shape=(grad_s...  2.42 us

profile of v4, /device:TPU:1, one launch (start us, length us, event | category | flops | bytes accessed | tf_op | source)
XLA Modules:
  0.0 42.5 jit_solution(13935985464634197269)
XLA Ops:
  0.6 39.5 %hyena_backward.1 = (bf16[2,64,8,256]{3,2,1,0:T(8,128)(2,1)}, f32[3,768]{1,0:T(4,128)}, bf16[256,128]{1,0:T(8,128)(2,1)}, f32[256,128]{1,0:T(8,128)}, f32[256,128]{1,0:T(8,128)}) custom-call(bf16[256,128]{1,0:T(8,128)(2,1)} %feat_in.1, s32[1,128]{1,0:T(1,128)} %order_in.1, bf16[256,128]{1,0:T(8,128)(2,1)} %cot_in.1, bf16[768,256]{1,0:T(8,128)(2,1)} %win_in.1, ...), custom_call_target="tpu_custom_call" | custom-call | tf_op jit(solution)/shard_map/hyena_backward/pallas_call | solution.py:593
  40.1 2.4 %row_order.1 = (bf16[256,128]{1,0:T(8,128)(2,1)}, f32[768,256]{1,0:T(8,128)}, f32[256,256]{1,0:T(8,128)}, f32[3,768]{1,0:T(4,128)}, f32[256,128]{1,0:T(8,128)}, /*index=5*/f32[256,128]{1,0:T(8,128)}) custom-call(bf16[2,64,8,256]{3,2,1,0:T(8,128)(2,1)} %get-tuple-element.17.sums_in, f32[3,768]{1,0:T(4,128)} %get-tuple-element.18.short_in, ...), custom_call_target="tpu_custom_call" | custom-call | tf_op jit(solution)/shard_map/row_order/pallas_call | solution.py:650

commit v5 on v4

--- a/solution.py
+++ b/solution.py
@@ -23,7 +23,7 @@
 
 def chip_offsets():
     steps = [(a, b, c) for a in range(SIDE) for b in range(SIDE) for c in range(SIDE) if a + b + c]
-    return sorted(steps, key=lambda step: -hops(step))
+    return sorted(steps, key=lambda step: (-hops(step), tuple(-min(d, SIDE - d) for d in step)))
 
 
 def plane_offsets():
@@ -136,22 +136,23 @@
 
     seq_index = lax.axis_index("seq")
     fft_index = lax.axis_index("fft")
-    core = fft_index % 2
-    x = (fft_index // 2) % 2 * 2 + seq_index // SIDE
-    y = fft_index // SIDE
-    z = seq_index % SIDE
-    along_x = [(x + d) % SIDE % 2 * 32 + (x + d) % SIDE // 2 for d in range(SIDE)]
-    along_y = [(y + d) % SIDE * 2 for d in range(SIDE)]
-    along_z = [(z + d) % SIDE * 8 for d in range(SIDE)]
+    core = lax.rem(fft_index, 2)
+    x = lax.rem(lax.div(fft_index, 2), 2) * 2 + lax.div(seq_index, SIDE)
+    y = lax.div(fft_index, SIDE)
+    z = lax.rem(seq_index, SIDE)
+    turned_x, turned_y, turned_z = ([lax.rem(p + d, SIDE) for d in range(SIDE)] for p in (x, y, z))
+    along_x = [lax.rem(p, 2) * 32 + lax.div(p, 2) for p in turned_x]
+    along_y = [p * 2 for p in turned_y]
+    along_z = [p * 8 for p in turned_z]
     chip = along_x[0] + along_y[0] + along_z[0]
     me = 2 * chip + core
     sibling = 2 * chip + (1 - core)
     other_chips = [along_x[a] + along_y[b] + along_z[c] for a, b, c in chip_offsets()]
-    in_line = [(x + d) % SIDE % 2 * 2 + (x + d) % SIDE // 2 for d in range(SIDE)]
+    in_line = [lax.rem(p, 2) * 2 + lax.div(p, 2) for p in turned_x]
     line_chips = [along_x[d] + along_y[0] + along_z[0] for d in range(SIDE)]
     here = z * SIDE + y
     plane = [
-        ((z + c) % SIDE * SIDE + (y + b) % SIDE, along_x[0] + along_y[b] + along_z[c])
+        (turned_z[c] * SIDE + turned_y[b], along_x[0] + along_y[b] + along_z[c])
         for _, b, c in plane_offsets()
     ]
     mine = in_line[0]
@@ -378,7 +379,6 @@
             part = jnp.sum(part, axis=1, keepdims=True)
             line = jnp.where(short_lane == 3 * j + k, part * scale, line)
     short_slab[...] = line
-    exchange(lambda peer_chip: short_slab, shorts.at[core, chip], 2)
     grads = backward(
         [conj_times(spec_value[c], spec_gfm[c]) for c in range(2)]
         + [conj_times(spec_fo[c], spec_gsm[c]) for c in range(2)]
@@ -409,14 +409,13 @@
     partial = jnp.where(kind < 6, with_seq, with_cot) * scale
     send3[...] = partial.reshape(SIDE * SIDE, 8, 256).astype(bf16)
     plane_exchange(send3, recv3, 3)
+    exchange(lambda peer_chip: short_slab, shorts.at[core, chip], 2)
     own_rows = rows_line.at[mine, core]
     for d in (2, 1, 3):
         for c in range(2):
             send(recv2.at[:, SIDE * c + in_line[d]], own_rows, 7, 2 * line_chips[d] + c)
     send(recv2.at[:, SIDE * (1 - core) + mine], own_rows, 7, sibling)
     pltpu.make_async_copy(recv2.at[:, SIDE * core + mine], own_rows, recv_sem.at[7]).start()
-    arrived(shorts.at[core], 2)
-    shorts_to_sibling = send(shorts.at[core], shorts.at[core], 9, sibling)
 
     arrived(recv3, 3)
     slab[...] = jnp.sum(recv3[...].astype(f32), axis=0).astype(bf16)
@@ -437,6 +436,8 @@
     send(slab, own_sums, 10, sibling)
     pltpu.make_async_copy(slab, own_sums, recv_sem.at[10]).start()
 
+    arrived(shorts.at[core], 2)
+    shorts_to_sibling = send(shorts.at[core], shorts.at[core], 9, sibling)
     arrived(rows_line, 7)
     by_place = [
         jnp.stack([rows_line[k, p].astype(f32) for p in range(2)], axis=1) for k in range(SIDE)

time: 42.7 us -> 42.5 us (level)
  no operation moved by 1% of the time
where the time goes in v5:
time: 42.5 us; the launch traced here: 42.3 us
  Pallas kernels  41.7 us (98%)
  between operations  0.64 us (2%)
    pallas_call x1, Pallas kernels, local(): pl.pallas_call(functools.partial(kernel, count), out_shape=(shape((2, chi...  39.3 us
    pallas_call x1, Pallas kernels, local(): pl.pallas_call(functools.partial(finish_kernel, count), out_shape=(grad_s...  2.42 us

profile of v5, /device:TPU:1, one launch (start us, length us, event | category | flops | bytes accessed | tf_op | source)
XLA Modules:
  0.0 42.3 jit_solution(6399033448409263575)
XLA Ops:
  0.6 39.3 %hyena_backward.1 = (bf16[2,64,8,256]{3,2,1,0:T(8,128)(2,1)}, f32[3,768]{1,0:T(4,128)}, bf16[256,128]{1,0:T(8,128)(2,1)}, f32[256,128]{1,0:T(8,128)}, f32[256,128]{1,0:T(8,128)}) custom-call(bf16[256,128]{1,0:T(8,128)(2,1)} %feat_in.1, s32[1,128]{1,0:T(1,128)} %order_in.1, bf16[256,128]{1,0:T(8,128)(2,1)} %cot_in.1, bf16[768,256]{1,0:T(8,128)(2,1)} %win_in.1, ...), custom_call_target="tpu_custom_call" | custom-call | tf_op jit(solution)/shard_map/hyena_backward/pallas_call | solution.py:594
  39.9 2.4 %row_order.1 = (bf16[256,128]{1,0:T(8,128)(2,1)}, f32[768,256]{1,0:T(8,128)}, f32[256,256]{1,0:T(8,128)}, f32[3,768]{1,0:T(4,128)}, f32[256,128]{1,0:T(8,128)}, /*index=5*/f32[256,128]{1,0:T(8,128)}) custom-call(bf16[2,64,8,256]{3,2,1,0:T(8,128)(2,1)} %get-tuple-element.17.sums_in, f32[3,768]{1,0:T(4,128)} %get-tuple-element.18.short_in, ...), custom_call_target="tpu_custom_call" | custom-call | tf_op jit(solution)/shard_map/row_order/pallas_call | solution.py:651

commit v6 on v5

--- a/solution.py
+++ b/solution.py
@@ -285,15 +285,17 @@
     lane_id = lax.broadcasted_iota(jnp.int32, (blocks, lanes), 1)
     row_id = lax.broadcasted_iota(jnp.int32, (blocks, lanes), 0)
 
-    def earlier(x, steps):
-        turned = pltpu.roll(x, steps, 1)
-        above = jnp.where(row_id == 0, 0.0, pltpu.roll(turned, 1, 0))
-        return jnp.where(lane_id < steps, above, turned)
-
-    def later(x, steps):
-        turned = pltpu.roll(x, lanes - steps, 1)
-        below = jnp.where(row_id == blocks - 1, 0.0, pltpu.roll(turned, blocks - 1, 0))
-        return jnp.where(lane_id >= lanes - steps, below, turned)
+    def earlier(x):
+        above = jnp.where(row_id == 0, 0.0, pltpu.roll(x, 1, 0))
+        return [
+            pltpu.roll(jnp.where(lane_id >= lanes - k, above, x), k, 1) for k in range(1, 3)
+        ]
+
+    def later(x):
+        below = jnp.where(row_id == blocks - 1, 0.0, pltpu.roll(x, blocks - 1, 0))
+        return [
+            pltpu.roll(jnp.where(lane_id < k, below, x), lanes - k, 1) for k in range(1, 3)
+        ]
 
     filters = [
         ref[pl.ds(c, count, stride=2), :] for ref in (filt1_ref, filt2_ref) for c in range(2)
@@ -312,16 +314,14 @@
     def tap(s, c, k):
         return taps_ref[k, width * s + 2 * me + c]
 
-    shifted = []
     streams = []
     for s in range(3):
         for c in range(2):
             now = stage_b[pl.ds(2 * s + c, count, stride=8), :]
-            moved = [now, earlier(now, 1), earlier(now, 2)]
+            moved = [now, *earlier(now)]
             mixed = tap(s, c, 0) * now
             for k in range(1, 3):
                 mixed = mixed + tap(s, c, k) * moved[k]
-            shifted.append(moved)
             streams.append(mixed.astype(bf16).astype(f32))
     value, gate_one, gate_two = streams[0:2], streams[2:4], streams[4:6]
     out_grad = [stage_b[pl.ds(6 + c, count, stride=8), :] for c in range(2)]
@@ -352,8 +352,8 @@
         for c in range(2):
             g = grad_streams[2 * s + c]
             total = tap(s, c, 0) * g
-            for k in range(1, 3):
-                total = total + tap(s, c, k) * later(g, k)
+            for k, moved in enumerate(later(g), 1):
+                total = total + tap(s, c, k) * moved
             stage_a[pl.ds(2 * s + c, count, stride=8), :] = total
     for c in range(2):
         stage_a[pl.ds(6 + c, count, stride=8), :] = gate_two[c] * second_mix[c]
@@ -374,8 +374,9 @@
     line = jnp.zeros((1, lanes), f32)
     short_lane = lax.broadcasted_iota(jnp.int32, (1, lanes), 1)
     for j in range(6):
-        for k in range(3):
-            part = jnp.sum(grad_streams[j] * shifted[j][k], axis=0, keepdims=True)
+        now = stage_b[pl.ds(j, count, stride=8), :]
+        for k, moved in enumerate([now, *earlier(now)]):
+            part = jnp.sum(grad_streams[j] * moved, axis=0, keepdims=True)
             part = jnp.sum(part, axis=1, keepdims=True)
             line = jnp.where(short_lane == 3 * j + k, part * scale, line)
     short_slab[...] = line
@@ -531,7 +532,8 @@
         pltpu.make_async_copy(source, target, in_sem.at[n])
         for n, (source, target) in enumerate(
             (
-                (sums_in, sums_ref),
+                (sums_in.at[:, :, :, pl.ds(0, lanes)], sums_ref.at[0]),
+                (sums_in.at[:, :, :, pl.ds(lanes, lanes)], sums_ref.at[1]),
                 (short_in, gshort_ref),
                 (gf1_in, gf1_ref),
                 (gf2_in, gf2_ref),
@@ -548,10 +550,10 @@
         copy.start()
         stores.append(copy)
 
-    loads[0].wait()
     for h in range(2):
+        loads[h].wait()
         part = pl.ds(h * lanes, lanes)
-        stage[...] = sums_ref[:, :, :, part].astype(f32).reshape(count * 8, lanes)
+        stage[...] = sums_ref[h].astype(f32).reshape(count * 8, lanes)
         for half in range(2):
             for s in range(4):
                 for c in range(2):
@@ -562,9 +564,9 @@
         gwout_ref[part, :] = ordered[h, 3 * width : 4 * width, :].T
         store(gwout_ref.at[part], gwout_out.at[part])
     for n, (ref, target) in enumerate(((gf1_ref, gf1_out), (gf2_ref, gf2_out), (gfeat_ref, gfeat_out))):
-        loads[2 + n].wait()
+        loads[3 + n].wait()
         store(ref, target)
-    loads[1].wait()
+    loads[2].wait()
     store(gshort_ref, gshort_out)
     for copy in stores:
         copy.wait()
@@ -660,7 +662,7 @@
         in_specs=[anywhere] * 5,
         out_specs=(anywhere,) * 6,
         scratch_shapes=[
-            pltpu.VMEM((2, chips, 8, width), bf16),
+            pltpu.VMEM((2, 2, chips, 8, lanes), bf16),
             pltpu.VMEM((width, lanes), bf16),
             pltpu.VMEM((width, lanes), f32),
             pltpu.VMEM((width, lanes), f32),
@@ -668,7 +670,7 @@
             pltpu.VMEM((3, 3 * width), f32),
             pltpu.VMEM((2, 8 * count, lanes), f32),
             pltpu.VMEM((8 * count, lanes), f32),
-            pltpu.SemaphoreType.DMA((5,)),
+            pltpu.SemaphoreType.DMA((6,)),
             pltpu.SemaphoreType.DMA((8,)),
         ],
         name="row_order",

time: 42.5 us -> 42.4 us (level)
  no operation moved by 1% of the time
where the time goes in v6:
time: 42.4 us; the launch traced here: 42.2 us
  Pallas kernels  41.6 us (98%)
  between operations  0.64 us (2%)
    pallas_call x1, Pallas kernels, local(): pl.pallas_call(functools.partial(kernel, count), out_shape=(shape((2, chi...  39.3 us
    pallas_call x1, Pallas kernels, local(): pl.pallas_call(functools.partial(finish_kernel, count), out_shape=(grad_s...  2.31 us

profile of v6, /device:TPU:1, one launch (start us, length us, event | category | flops | bytes accessed | tf_op | source)
XLA Modules:
  0.0 42.2 jit_solution(6757206523386695867)
XLA Ops:
  0.6 39.3 %hyena_backward.1 = (bf16[2,64,8,256]{3,2,1,0:T(8,128)(2,1)}, f32[3,768]{1,0:T(4,128)}, bf16[256,128]{1,0:T(8,128)(2,1)}, f32[256,128]{1,0:T(8,128)}, f32[256,128]{1,0:T(8,128)}) custom-call(bf16[256,128]{1,0:T(8,128)(2,1)} %feat_in.1, s32[1,128]{1,0:T(1,128)} %order_in.1, bf16[256,128]{1,0:T(8,128)(2,1)} %cot_in.1, bf16[768,256]{1,0:T(8,128)(2,1)} %win_in.1, ...), custom_call_target="tpu_custom_call" | custom-call | tf_op jit(solution)/shard_map/hyena_backward/pallas_call | solution.py:596
  39.9 2.3 %row_order.1 = (bf16[256,128]{1,0:T(8,128)(2,1)}, f32[768,256]{1,0:T(8,128)}, f32[256,256]{1,0:T(8,128)}, f32[3,768]{1,0:T(4,128)}, f32[256,128]{1,0:T(8,128)}, /*index=5*/f32[256,128]{1,0:T(8,128)}) custom-call(bf16[2,64,8,256]{3,2,1,0:T(8,128)(2,1)} %get-tuple-element.17.sums_in, f32[3,768]{1,0:T(4,128)} %get-tuple-element.18.short_in, ...), custom_call_target="tpu_custom_call" | custom-call | tf_op jit(solution)/shard_map/row_order/pallas_call | solution.py:653

commit v7 on v6

--- a/solution.py
+++ b/solution.py
@@ -247,9 +247,12 @@
     second_back = (tab_ref[768:1024, :], tab_ref[1024:1280, :])
     first_back = (tab_ref[1280:1408, :], tab_ref[1408:1536, :])
 
-    def forward(signals):
+    def forward(signals, exact=0):
         high, low = halves(jnp.concatenate(signals, axis=1))
-        mid = dot(first, jnp.concatenate([high, high], axis=0)) + dot(first[:, 0:lanes], low)
+        mid = dot(first, jnp.concatenate([high, high], axis=0))
+        rest = exact * lanes
+        tail = mid[:, rest:] + dot(first[:, 0:lanes], low[:, rest:])
+        mid = jnp.concatenate([mid[:, 0:rest], tail], axis=1) if exact else tail
         rows = []
         for i in range(len(signals)):
             re = mid[0:blocks, i * lanes : (i + 1) * lanes]
@@ -327,7 +330,7 @@
     out_grad = [stage_b[pl.ds(6 + c, count, stride=8), :] for c in range(2)]
     grad_second_mix = [out_grad[c] * gate_two[c] for c in range(2)]
 
-    spec = forward(value + grad_second_mix)
+    spec = forward(value + grad_second_mix, exact=2)
     spec_value, spec_gsm = spec[0:2], spec[2:4]
     mixes = backward(
         [times(spec_f1[c], spec_value[c]) for c in range(2)]

time: 42.4 us -> 42.5 us (level)
  no operation moved by 1% of the time
where the time goes in v7:
time: 42.5 us; the launch traced here: 42.4 us
  Pallas kernels  41.7 us (98%)
  between operations  0.64 us (2%)
    pallas_call x1, Pallas kernels, local(): pl.pallas_call(functools.partial(kernel, count), out_shape=(shape((2, chi...  39.4 us
    pallas_call x1, Pallas kernels, local(): pl.pallas_call(functools.partial(finish_kernel, count), out_shape=(grad_s...  2.31 us

profile of v7, /device:TPU:1, one launch (start us, length us, event | category | flops | bytes accessed | tf_op | source)
XLA Modules:
  0.0 42.4 jit_solution(2778209527791810197)
XLA Ops:
  0.6 39.4 %hyena_backward.1 = (bf16[2,64,8,256]{3,2,1,0:T(8,128)(2,1)}, f32[3,768]{1,0:T(4,128)}, bf16[256,128]{1,0:T(8,128)(2,1)}, f32[256,128]{1,0:T(8,128)}, f32[256,128]{1,0:T(8,128)}) custom-call(bf16[256,128]{1,0:T(8,128)(2,1)} %feat_in.1, s32[1,128]{1,0:T(1,128)} %order_in.1, bf16[256,128]{1,0:T(8,128)(2,1)} %cot_in.1, bf16[768,256]{1,0:T(8,128)(2,1)} %win_in.1, ...), custom_call_target="tpu_custom_call" | custom-call | tf_op jit(solution)/shard_map/hyena_backward/pallas_call | solution.py:599
  40.1 2.3 %row_order.1 = (bf16[256,128]{1,0:T(8,128)(2,1)}, f32[768,256]{1,0:T(8,128)}, f32[256,256]{1,0:T(8,128)}, f32[3,768]{1,0:T(4,128)}, f32[256,128]{1,0:T(8,128)}, /*index=5*/f32[256,128]{1,0:T(8,128)}) custom-call(bf16[2,64,8,256]{3,2,1,0:T(8,128)(2,1)} %get-tuple-element.17.sums_in, f32[3,768]{1,0:T(4,128)} %get-tuple-element.18.short_in, ...), custom_call_target="tpu_custom_call" | custom-call | tf_op jit(solution)/shard_map/row_order/pallas_call | solution.py:656
